TPU v7x, 32 devices: a whole 2x2x4 slice. The times are simulated.
32 devices in a mesh: gx: 4 (over x, core), gy: 8 (over z, y).
Axes of the slice: x: 2, y: 2, z: 4, core: 2. Of those that a mesh axis runs over, the one named last changes fastest.
Arguments:
- state_field: float32 [128, 128, 16, 256], P('gx', 'gy'), may hold values from -80 to 80
- start_basis: float32 [256, 32], replicated, may hold values from -6 to 6
Outputs:
- core_tensor: float32 [128, 128, 512], P('gx', 'gy')
- z_factor: float32 [256, 32], replicated
- x_triangle: float32 [128, 128], replicated
All inputs are finite; a program needn't handle non-finite values.
Results may differ from a plain program's by a relative error of at most 0.0003.
Values sent between devices are 32-bit elements; how exact they have to be, the bound alone decides.
No kernel may reach another device: no remote copies, remote signals or barrier semaphores. Data moves between devices by JAX's collectives and lax.ppermute only.
A program may use at most 64 MiB of HBM per device.

v0:
```python
import jax
import jax.numpy as jnp
from jax import lax
from jax.sharding import PartitionSpec as P

ITERS = 3


precise = lax.Precision.HIGHEST


def orthonormal(image):
    for repeat in range(2):
        inner_gram = jnp.dot(image.T, image, precision=precise, preferred_element_type=jnp.float32)
        lower_factor = jnp.linalg.cholesky(inner_gram)
        image = lax.linalg.triangular_solve(
            lower_factor, image, left_side=False, lower=True, transpose_a=True
        )
    return image


def local(state_field, start_basis):
    x_cells, y_cells, species, z_cells = state_field.shape
    unfolded = state_field.reshape(x_cells * y_cells * species, z_cells)
    local_gram = lax.dot_general(
        unfolded,
        unfolded,
        (((0,), (0,)), ((), ())),
        precision=precise,
        preferred_element_type=jnp.float32,
    )
    z_basis = start_basis
    gram_z = lax.psum(local_gram, ("gx", "gy"))
    for iteration in range(ITERS):
        z_basis = orthonormal(
            jnp.dot(gram_z, z_basis, precision=precise, preferred_element_type=jnp.float32)
        )
    rank_kept = z_basis.shape[1]
    core_rows = jnp.dot(unfolded, z_basis, precision=precise, preferred_element_type=jnp.float32)
    core_tensor = core_rows.reshape(x_cells, y_cells, species * rank_kept)
    own_rows = core_tensor.reshape(x_cells, -1)
    row_piece = lax.all_gather(core_tensor, "gx", axis=0, tiled=True)
    piece_rows = row_piece.reshape(row_piece.shape[0], -1)
    product = jnp.dot(own_rows, piece_rows.T, precision=precise, preferred_element_type=jnp.float32)
    summed_row = lax.psum(product, "gy")
    gram_x = lax.all_gather(summed_row, "gx", axis=0, tiled=True)
    column_count = y_cells * lax.axis_size("gy") * species * rank_kept
    x_triangle = jnp.linalg.cholesky(gram_x).T / jnp.sqrt(jnp.float32(column_count))
    return (core_tensor, z_basis, x_triangle)


def solution(mesh):
    return jax.shard_map(
        local,
        mesh=mesh,
        in_specs=(P("gx", "gy", None, None), P()),
        out_specs=(P("gx", "gy", None), P(), P()),
        check_vma=False,
    )
```

profile of v0, /device:TPU:0, one launch (start us, length us, event | category | flops | bytes accessed | tf_op | source)
XLA Modules:
  0.0 325.5 jit_solution(4373195180380664984)
XLA Ops:
  7.2 17.8 %convolution_bitcast_fusion.1 = f32[256,256]{1,0:T(8,128)} fusion(f32[32,16,16,256]{3,2,1,0:T(8,128)} %param.5), kind=kOutput, calls=%fused_computation.1 | convolution fusion | flops 6442450944 | bytes 8650752 | tf_op jit(solution)/shard_map/dot_general | solution.py:25
  25.3 129.2 %all-reduce.2.cloned.1.call-done = f32[256,256]{1,0:T(8,128)} async-done(((f32[256,256]{1,0:T(8,128)}), f32[256,256]{1,0:T(8,128)}) %all-reduce.2.cloned.1.call-update) | async-done | bytes 262160 | tf_op jit(solution)/shard_map/psum | solution.py:33
  154.5 1.3 fusion.29
  156.1 2.9 cholesky.142
  159.0 0.6 compare_reduce_fusion.5
  159.7 0.7 fusion.1
  160.3 2.4 custom-call.13
  162.7 0.2 convolution_bitcast_fusion.7
  163.2 2.9 cholesky.153
  166.2 0.6 compare_reduce_fusion.4
  166.8 0.7 fusion.2
  167.5 2.4 custom-call.14
  169.9 0.2 convolution_bitcast_fusion.6
  170.2 1.3 fusion.32
  171.7 2.9 cholesky.164
  174.7 0.6 compare_reduce_fusion.3
  175.3 0.7 fusion.3
  176.0 2.4 custom-call.15
  178.4 0.2 convolution_bitcast_fusion.5
  178.9 2.9 cholesky.175
  181.9 0.6 compare_reduce_fusion.2
  182.5 0.7 fusion.4
  183.2 2.4 custom-call.16
  185.6 0.2 convolution_bitcast_fusion.4
  185.9 1.3 fusion.35
  187.4 2.9 cholesky.186
  190.4 0.6 compare_reduce_fusion.1
  191.0 0.7 fusion.5
  191.7 2.4 custom-call.17
  194.1 0.2 convolution_bitcast_fusion.3
  194.6 2.9 cholesky.197
  197.6 0.6 compare_reduce_fusion
  198.2 0.7 fusion.6
  198.9 2.4 custom-call.18
  201.3 0.2 convolution_bitcast_fusion.2
  201.6 10.1 %convolution_bitcast_fusion = f32[8192,32]{0,1:T(8,128)S(1)} fusion(f32[256,32]{0,1:T(8,128)S(1)} %convolution_bitcast_fusion.2, f32[8192,256]{1,0:T(8,128)} %bitcast.112), kind=kOutput, calls=%fused_computation | convolution fusion | flops 805306368 | bytes 9469952 | tf_op jit(solution)/shard_map/dot_general | solution.py:39
  211.7 2.7 copy.35
  214.3 4.4 %reshape.33 = f32[32,16,512]{2,1,0:T(8,128)} reshape(f32[8192,32]{1,0:T(8,128)} %copy.35) | data formatting | bytes 2097152 | tf_op jit(solution)/shard_map/reshape | solution.py:40
  218.8 3.5 %reshape_reshape.3 = f32[32,8192]{1,0:T(8,128)S(1)} reshape(f32[8192,32]{1,0:T(8,128)} %copy.35) | data formatting | bytes 2097152 | tf_op jit(solution)/shard_map/reshape;reshape | solution.py:41
  222.3 30.1 %all-gather.2.cloned.1.call-done = f32[128,16,512]{2,1,0:T(8,128)} async-done(((f32[32,16,512]{2,1,0:T(8,128)}), f32[128,16,512]{2,1,0:T(8,128)}) %all-gather.2.cloned.1.call-update) | async-done | bytes 4194320 | tf_op jit(solution)/shard_map/all_gather | solution.py:42
  252.4 5.6 %copy.40 = f32[16,8,16,512]{3,1,2,0:T(8,128)S(1)} copy(f32[16,8,16,512]{3,2,1,0:T(8,128)} %bitcast.113) | data formatting | bytes 8388608
  258.0 4.1 %fusion.38 = f32[32,128]{1,0:T(8,128)S(1)} fusion(f32[32,8192]{1,0:T(8,128)S(1)} %reshape_reshape.3, f32[128,8192]{1,0:T(8,128)S(1)} %bitcast.111), kind=kOutput, calls=%fused_computation.73 | convolution fusion | flops 402653184 | bytes 5259264 | tf_op jit(solution)/shard_map/dot_general | solution.py:44
  262.2 37.1 %psum.15 = f32[32,128]{1,0:T(8,128)S(1)} all-reduce(f32[32,128]{1,0:T(8,128)S(1)} %fusion.38), channel_id=1, replica_groups=mesh['gx'=4,'gy'=8] {'gy'}, use_global_device_ids=true, to_apply=%region_3.6 | all-reduce | flops 4096 | bytes 32768 | tf_op jit(solution)/shard_map/psum | solution.py:45
  299.2 5.5 %all_gather.7 = f32[128,128]{1,0:T(8,128)S(1)} all-gather(f32[32,128]{1,0:T(8,128)S(1)} %psum.15), channel_id=1, replica_groups=mesh['gx'=4,'gy'=8] {'gx'}, dimensions={0}, use_global_device_ids=true | all-gather | bytes 81920 | tf_op jit(solution)/shard_map/all_gather | solution.py:46
  304.8 11.7 %cholesky.45 = f32[128,128]{1,0:T(8,128)S(1)} custom-call(f32[128,128]{1,0:T(8,128)S(1)} %fusion), custom_call_target="Cholesky" | custom-call | tf_op jit(solution)/shard_map/jit(cholesky)/cholesky | solution.py:48
  316.6 0.6 compare_reduce_fusion.6
  317.2 0.7 multiply_bitcast_fusion
  317.9 0.7 copy.38
  (35 shorter events, 2.1 us)
Async XLA Ops:
  7.2 147.3 %copy-start = (f32[256,32]{0,1:T(8,128)S(1)}, f32[256,32]{0,1:T(8,128)}, u32[]{:S(2)}) copy-start(f32[256,32]{0,1:T(8,128)} %param.6) | copy-start | bytes 98308
  7.2 147.3 %all-reduce.2.cloned.1.call-start = ((), (), s32[]{:S(2)}) async-start(), calls=%async_computation | async-start | bytes 524288 | tf_op jit(solution)/shard_map/psum | solution.py:33
  25.0 227.4 %all-gather.2.cloned.1.call-start = ((), (), s32[]{:S(2)}) async-start(), calls=%async_computation.1 | async-start | bytes 5242880 | tf_op jit(solution)/shard_map/all_gather | solution.py:42
  201.6 17.2 %copy-start.1 = (f32[256,32]{0,1:T(8,128)}, f32[256,32]{0,1:T(8,128)S(1)}, u32[]{:S(2)}) copy-start(f32[256,32]{0,1:T(8,128)S(1)} %convolution_bitcast_fusion.2) | copy-start | bytes 98308
Sparse Core Ops, SparseCore 0:
  25.2 129.2 all-reduce.1
  218.9 33.4 all-gather.1
where the time goes:
time: 326 us; the launch traced here: 325 us
  waiting for transfers between devices  159 us (49%)
  other arithmetic  53.2 us (16%)
  blocking collectives  42.6 us (13%)
  matrix products  38.3 us (12%)
  local copies, waits for them, and re-layouts  17.4 us (5%)
  between operations  14.3 us (4%)
    psum x1, waiting for transfers between devices, local(): gram_z = lax.psum(local_gram, ('gx', 'gy'))  129 us
    psum x1, blocking collectives, local(): summed_row = lax.psum(product, 'gy')  37.1 us
    all_gather x1, waiting for transfers between devices, local(): row_piece = lax.all_gather(core_tensor, 'gx', axis=0, tiled=True)  30.1 us
    another operation x18, other arithmetic, orthonormal(): lower_factor = jnp.linalg.cholesky(inner_gram)  21.6 us
    another operation x12, other arithmetic, orthonormal(): lax.linalg.triangular_solve(lower_factor, image, left_side=False, lower=T...  18.5 us
    dot_general x1, matrix products, local(): lax.dot_general(unfolded, unfolded, (((0,), (0,)), ((), ())), precision=p...  17.8 us
    another operation x3, other arithmetic, local(): jnp.linalg.cholesky(gram_x).T / jnp.sqrt(jnp.float32(column_count))  12.4 us
    dot_general x1, matrix products, local(): jnp.dot(unfolded, z_basis, precision=precise, preferred_element_type=jnp....  10.1 us
  transfers between devices with their start and end apart: 2, of which 2 were waited for; matrix products, arithmetic and copies ran while one was open for 1% of the time, Pallas kernels for 0%

commit v1 on v0

--- a/solution.py
+++ b/solution.py
@@ -7,6 +7,45 @@
 
 
 precise = lax.Precision.HIGHEST
+triple = lax.Precision.HIGH
+
+
+def bits(size):
+    return [1 << b for b in range(size.bit_length() - 1)]
+
+
+def partner(value, axis, bit):
+    size = lax.axis_size(axis)
+    return lax.ppermute(value, axis, [(i, i ^ bit) for i in range(size)])
+
+
+def summed(value, skip_core=False):
+    for axis in ("gx", "gy"):
+        size = lax.axis_size(axis)
+        if size & (size - 1):
+            value = lax.psum(value, axis)
+            continue
+        for bit in bits(size)[1 if skip_core and axis == "gx" else 0 :]:
+            value = value + partner(value, axis, bit)
+    return value
+
+
+def sum_gram(gram):
+    half = gram.shape[0] // 2
+    quarter = half // 2
+    a, b, c = gram[:half, :half], gram[:half, half:], gram[half:, half:]
+    first = jnp.concatenate([a, b[:quarter]])
+    second = jnp.concatenate([c, b[quarter:]])
+    upper = lax.axis_index("gx") % 2 == 0
+    mine = jnp.where(upper, first, second)
+    other = jnp.where(upper, second, first)
+    mine = mine + partner(other, "gx", 1)
+    mine = summed(mine, skip_core=True)
+    other = partner(mine, "gx", 1)
+    first = jnp.where(upper, mine, other)
+    second = jnp.where(upper, other, mine)
+    b = jnp.concatenate([first[half:], second[half:]])
+    return jnp.block([[first[:half], b], [b.T, second[:half]]])
 
 
 def orthonormal(image):
@@ -26,24 +65,23 @@
         unfolded,
         unfolded,
         (((0,), (0,)), ((), ())),
-        precision=precise,
+        precision=triple,
         preferred_element_type=jnp.float32,
     )
     z_basis = start_basis
-    gram_z = lax.psum(local_gram, ("gx", "gy"))
+    gram_z = sum_gram(local_gram)
     for iteration in range(ITERS):
         z_basis = orthonormal(
             jnp.dot(gram_z, z_basis, precision=precise, preferred_element_type=jnp.float32)
         )
     rank_kept = z_basis.shape[1]
-    core_rows = jnp.dot(unfolded, z_basis, precision=precise, preferred_element_type=jnp.float32)
+    core_rows = jnp.dot(unfolded, z_basis, precision=triple, preferred_element_type=jnp.float32)
     core_tensor = core_rows.reshape(x_cells, y_cells, species * rank_kept)
-    own_rows = core_tensor.reshape(x_cells, -1)
-    row_piece = lax.all_gather(core_tensor, "gx", axis=0, tiled=True)
-    piece_rows = row_piece.reshape(row_piece.shape[0], -1)
-    product = jnp.dot(own_rows, piece_rows.T, precision=precise, preferred_element_type=jnp.float32)
-    summed_row = lax.psum(product, "gy")
-    gram_x = lax.all_gather(summed_row, "gx", axis=0, tiled=True)
+    x_parts = lax.axis_size("gx")
+    by_part = core_tensor.reshape(x_cells, x_parts, -1).transpose(1, 0, 2)
+    all_x = lax.all_to_all(by_part, "gx", 0, 0).reshape(x_parts * x_cells, -1)
+    product = jnp.dot(all_x, all_x.T, precision=triple, preferred_element_type=jnp.float32)
+    gram_x = summed(product)
     column_count = y_cells * lax.axis_size("gy") * species * rank_kept
     x_triangle = jnp.linalg.cholesky(gram_x).T / jnp.sqrt(jnp.float32(column_count))
     return (core_tensor, z_basis, x_triangle)

time: 326 us -> 149 us (0.46)
  waiting for transfers between devices: 159 us -> 26.1 us
  blocking collectives: 42.6 us -> 17 us
  starting transfers between devices: 0.26 us -> 15.9 us
  matrix products: 38.3 us -> 22.9 us
  between operations: 14.3 us -> 1.07 us
  local copies, waits for them, and re-layouts: 17.4 us -> 12.8 us
    psum x1 -> x0, waiting for transfers between devices: 129 us -> none  [local(): gram_z = lax.psum(local_gram, ('gx', 'gy'))]
    psum x1 -> x0, blocking collectives: 37.1 us -> none  [local(): summed_row = lax.psum(product, 'gy')]
    all_gather x1 -> x0, waiting for transfers between devices: 30.1 us -> none  [local(): row_piece = lax.all_gather(core_tensor, 'gx', axis=0, tiled=True)]
    ppermute x0 -> x11, waiting for transfers between devices: none -> 26.1 us  [partner(): return lax.ppermute(value, axis, [(i, i ^ bit) for i in range(size)])]
    all_to_all x0 -> x1, blocking collectives: none -> 17 us  [local(): all_x = lax.all_to_all(by_part, 'gx', 0, 0).reshape(x_parts * x_cells, -1)]
    ppermute x0 -> x11, starting transfers between devices: none -> 15.9 us  [partner(): return lax.ppermute(value, axis, [(i, i ^ bit) for i in range(size)])]
    dot_general x3, matrix products: 32 us -> 19.4 us  [the longest x1 11.8 us: local(): lax.dot_general(unfolded, unfolded, (((0,), (0,)), ((), ())), precision=t...]
    unnamed x6 -> x5, local copies, waits for them, and re-layouts: 6.34 us -> 0.75 us
  transfers between devices with their start and end apart: 2 -> 11, of which waited for: 2 -> 10; matrix products, arithmetic and copies ran while one was open for 1% -> 3% of each run, Pallas kernels for 0% -> 0%
where the time goes in v1:
time: 149 us
  other arithmetic  53.3 us (36%)
  waiting for transfers between devices  26.1 us (18%)
  matrix products  22.9 us (15%)
  blocking collectives  17 us (11%)
  starting transfers between devices  15.9 us (11%)
  local copies, waits for them, and re-layouts  12.8 us (9%)
    ppermute x11, waiting for transfers between devices, partner(): return lax.ppermute(value, axis, [(i, i ^ bit) for i in range(size)])  26.1 us
    another operation x18, other arithmetic, orthonormal(): lower_factor = jnp.linalg.cholesky(inner_gram)  21.6 us
    another operation x12, other arithmetic, orthonormal(): lax.linalg.triangular_solve(lower_factor, image, left_side=False, lower=T...  18.5 us
    all_to_all x1, blocking collectives, local(): all_x = lax.all_to_all(by_part, 'gx', 0, 0).reshape(x_parts * x_cells, -1)  17 us
    ppermute x11, starting transfers between devices, partner(): return lax.ppermute(value, axis, [(i, i ^ bit) for i in range(size)])  15.9 us
    another operation x3, other arithmetic, local(): jnp.linalg.cholesky(gram_x).T / jnp.sqrt(jnp.float32(column_count))  12.4 us
    dot_general x1, matrix products, local(): lax.dot_general(unfolded, unfolded, (((0,), (0,)), ((), ())), precision=t...  11.8 us
    dot_general x1, matrix products, local(): jnp.dot(unfolded, z_basis, precision=triple, preferred_element_type=jnp.f...  7.07 us
  transfers between devices with their start and end apart: 11, of which 10 were waited for; matrix products, arithmetic and copies ran while one was open for 3% of the time, Pallas kernels for 0%

profile of v1, /device:TPU:0, one launch (start us, length us, event | category | flops | bytes accessed | tf_op | source)
XLA Modules:
  0.0 149.1 jit_solution(12299817335364578662)
XLA Ops:
  0.7 11.8 %convolution_bitcast_fusion.1 = f32[256,256]{1,0:T(8,128)S(1)} fusion(f32[32,16,16,256]{3,2,1,0:T(8,128)} %param.5), kind=kOutput, calls=%fused_computation.1 | convolution fusion | flops 3221225472 | bytes 8650752 | tf_op jit(solution)/shard_map/dot_general | solution.py:64
  13.0 0.9 collective-permute-done
  14.0 2.9 %collective-permute-start.1 = (f32[192,128]{1,0:T(8,128)S(1)}, f32[192,128]{1,0:T(8,128)S(1)}, u32[]{:S(2)}, u32[]{:S(2)}) collective-permute-start(f32[192,128]{1,0:T(8,128)S(1)} %select_add_fusion), channel_id=1, source_target_pairs={{0,16},{8,24},{16,0},{24,8},{1,17},{9,25},{17,1},{25,9},{2,18},{10... | collective-permute-start | bytes 294920 | tf_op jit(solution)/shard_map/ppermute | solution.py:19
  16.9 3.1 %collective-permute-done.1 = f32[192,128]{1,0:T(8,128)S(1)} collective-permute-done((f32[192,128]{1,0:T(8,128)S(1)}, f32[192,128]{1,0:T(8,128)S(1)}, u32[]{:S(2)}, u32[]{:S(2)}) %collective-permute-start.1) | collective-permute-done | bytes 98336 | tf_op jit(solution)/shard_map/ppermute | solution.py:19
  20.0 1.8 %collective-permute-start.2 = (f32[192,128]{1,0:T(8,128)S(1)}, f32[192,128]{1,0:T(8,128)S(1)}, u32[]{:S(2)}, u32[]{:S(2)}) collective-permute-start(f32[192,128]{1,0:T(8,128)S(1)} %add.53), channel_id=1, source_target_pairs={{0,1},{1,0},{2,3},{3,2},{4,5},{5,4},{6,7},{7,6},{8,9},{9,8},{10,11... | collective-permute-start | bytes 294920 | tf_op jit(solution)/shard_map/ppermute | solution.py:19
  21.9 2.8 %collective-permute-done.2 = f32[192,128]{1,0:T(8,128)S(1)} collective-permute-done((f32[192,128]{1,0:T(8,128)S(1)}, f32[192,128]{1,0:T(8,128)S(1)}, u32[]{:S(2)}, u32[]{:S(2)}) %collective-permute-start.2) | collective-permute-done | bytes 98336 | tf_op jit(solution)/shard_map/ppermute | solution.py:19
  24.7 1.9 %collective-permute-start.3 = (f32[192,128]{1,0:T(8,128)S(1)}, f32[192,128]{1,0:T(8,128)S(1)}, u32[]{:S(2)}, u32[]{:S(2)}) collective-permute-start(f32[192,128]{1,0:T(8,128)S(1)} %add.54), channel_id=1, source_target_pairs={{0,2},{1,3},{2,0},{3,1},{4,6},{5,7},{6,4},{7,5},{8,10},{9,11},{10,... | collective-permute-start | bytes 294920 | tf_op jit(solution)/shard_map/ppermute | solution.py:19
  26.6 2.8 %collective-permute-done.3 = f32[192,128]{1,0:T(8,128)S(1)} collective-permute-done((f32[192,128]{1,0:T(8,128)S(1)}, f32[192,128]{1,0:T(8,128)S(1)}, u32[]{:S(2)}, u32[]{:S(2)}) %collective-permute-start.3) | collective-permute-done | bytes 98336 | tf_op jit(solution)/shard_map/ppermute | solution.py:19
  29.4 3.3 %collective-permute-start.4 = (f32[192,128]{1,0:T(8,128)S(1)}, f32[192,128]{1,0:T(8,128)S(1)}, u32[]{:S(2)}, u32[]{:S(2)}) collective-permute-start(f32[192,128]{1,0:T(8,128)S(1)} %add.55), channel_id=1, source_target_pairs={{0,4},{1,5},{2,6},{3,7},{4,0},{5,1},{6,2},{7,3},{8,12},{9,13},{10,... | collective-permute-start | bytes 294920 | tf_op jit(solution)/shard_map/ppermute | solution.py:19
  32.8 3.6 %collective-permute-done.4 = f32[192,128]{1,0:T(8,128)S(1)} collective-permute-done((f32[192,128]{1,0:T(8,128)S(1)}, f32[192,128]{1,0:T(8,128)S(1)}, u32[]{:S(2)}, u32[]{:S(2)}) %collective-permute-start.4) | collective-permute-done | bytes 98336 | tf_op jit(solution)/shard_map/ppermute | solution.py:19
  36.5 1.3 collective-permute-done.5
  38.6 2.9 %cholesky.142 = f32[32,32]{1,0:T(8,128)S(1)} custom-call(f32[32,32]{1,0:T(8,128)S(1)} %fusion.19), custom_call_target="Cholesky" | custom-call | tf_op jit(solution)/shard_map/jit(cholesky)/cholesky | solution.py:54
  41.6 0.6 compare_reduce_fusion.5
  42.2 0.7 fusion.2
  42.9 2.4 %custom-call.13 = f32[1,32,32]{1,2,0:T(8,128)S(1)} custom-call(f32[1,32,32]{2,1,0:T(8,128)S(1)} %fusion.2), custom_call_target="InvertDiagBlocksLowerTriangular" | custom-call | tf_op jit(solution)/shard_map/triangular_solve/custom-call.2 | solution.py:55
  45.8 2.9 %cholesky.153 = f32[32,32]{1,0:T(8,128)S(1)} custom-call(f32[32,32]{1,0:T(8,128)S(1)} %fusion.17), custom_call_target="Cholesky" | custom-call | tf_op jit(solution)/shard_map/jit(cholesky)/cholesky | solution.py:54
  48.7 0.6 compare_reduce_fusion.4
  49.4 0.7 fusion.3
  50.0 2.4 %custom-call.14 = f32[1,32,32]{1,2,0:T(8,128)S(1)} custom-call(f32[1,32,32]{2,1,0:T(8,128)S(1)} %fusion.3), custom_call_target="InvertDiagBlocksLowerTriangular" | custom-call | tf_op jit(solution)/shard_map/triangular_solve/custom-call.2 | solution.py:55
  53.3 2.9 %cholesky.164 = f32[32,32]{1,0:T(8,128)S(1)} custom-call(f32[32,32]{1,0:T(8,128)S(1)} %fusion.15), custom_call_target="Cholesky" | custom-call | tf_op jit(solution)/shard_map/jit(cholesky)/cholesky | solution.py:54
  56.3 0.6 compare_reduce_fusion.3
  56.9 0.7 fusion.4
  57.6 2.4 %custom-call.15 = f32[1,32,32]{1,2,0:T(8,128)S(1)} custom-call(f32[1,32,32]{2,1,0:T(8,128)S(1)} %fusion.4), custom_call_target="InvertDiagBlocksLowerTriangular" | custom-call | tf_op jit(solution)/shard_map/triangular_solve/custom-call.2 | solution.py:55
  60.5 2.9 %cholesky.175 = f32[32,32]{1,0:T(8,128)S(1)} custom-call(f32[32,32]{1,0:T(8,128)S(1)} %fusion.13), custom_call_target="Cholesky" | custom-call | tf_op jit(solution)/shard_map/jit(cholesky)/cholesky | solution.py:54
  63.5 0.6 compare_reduce_fusion.2
  64.1 0.7 fusion.5
  64.8 2.4 %custom-call.16 = f32[1,32,32]{1,2,0:T(8,128)S(1)} custom-call(f32[1,32,32]{2,1,0:T(8,128)S(1)} %fusion.5), custom_call_target="InvertDiagBlocksLowerTriangular" | custom-call | tf_op jit(solution)/shard_map/triangular_solve/custom-call.2 | solution.py:55
  68.1 2.9 %cholesky.186 = f32[32,32]{1,0:T(8,128)S(1)} custom-call(f32[32,32]{1,0:T(8,128)S(1)} %fusion.11), custom_call_target="Cholesky" | custom-call | tf_op jit(solution)/shard_map/jit(cholesky)/cholesky | solution.py:54
  71.7 0.7 fusion.6
  72.3 2.4 %custom-call.17 = f32[1,32,32]{1,2,0:T(8,128)S(1)} custom-call(f32[1,32,32]{2,1,0:T(8,128)S(1)} %fusion.6), custom_call_target="InvertDiagBlocksLowerTriangular" | custom-call | tf_op jit(solution)/shard_map/triangular_solve/custom-call.2 | solution.py:55
  75.3 2.9 %cholesky.197 = f32[32,32]{1,0:T(8,128)S(1)} custom-call(f32[32,32]{1,0:T(8,128)S(1)} %fusion.9), custom_call_target="Cholesky" | custom-call | tf_op jit(solution)/shard_map/jit(cholesky)/cholesky | solution.py:54
  78.9 0.7 fusion.7
  79.5 2.4 %custom-call.18 = f32[1,32,32]{1,2,0:T(8,128)S(1)} custom-call(f32[1,32,32]{2,1,0:T(8,128)S(1)} %fusion.7), custom_call_target="InvertDiagBlocksLowerTriangular" | custom-call | tf_op jit(solution)/shard_map/triangular_solve/custom-call.2 | solution.py:55
  82.2 7.1 %convolution_bitcast_fusion = f32[8192,32]{0,1:T(8,128)S(1)} fusion(f32[256,32]{0,1:T(8,128)S(1)} %convolution_bitcast_fusion.2, f32[8192,256]{1,0:T(8,128)} %bitcast.110), kind=kOutput, calls=%fused_computation | convolution fusion | flops 402653184 | bytes 9469952 | tf_op jit(solution)/shard_map/dot_general | solution.py:78
  89.3 2.6 %copy.41 = f32[8192,32]{1,0:T(8,128)} copy(f32[8192,32]{0,1:T(8,128)S(1)} %convolution_bitcast_fusion) | data formatting | bytes 2097152 | tf_op jit(solution)/shard_map/dot_general | solution.py:78
  91.9 3.8 %reshape_reshape.3 = f32[32,4,2048]{2,1,0:T(4,128)S(1)} reshape(f32[8192,32]{1,0:T(8,128)} %copy.41) | data formatting | bytes 2097152 | tf_op jit(solution)/shard_map/reshape;reshape | solution.py:81
  96.4 17.0 %all_to_all.5 = f32[4,32,2048]{2,1,0:T(8,128)S(1)} all-to-all(f32[4,32,2048]{2,1,0:T(8,128)S(1)} %copy.43), channel_id=1, replica_groups=mesh['gx'=4,'gy'=8] {'gx'}, dimensions={0} | all-to-all | bytes 2097152 | tf_op jit(solution)/shard_map/all_to_all | solution.py:82
  114.0 1.2 collective-permute-done.6
  115.7 3.9 %collective-permute-done.7 = f32[128,128]{0,1:T(8,128)S(1)} collective-permute-done((f32[128,128]{0,1:T(8,128)S(1)}, f32[128,128]{0,1:T(8,128)S(1)}, u32[]{:S(2)}, u32[]{:S(2)}) %collective-permute-start.7) | collective-permute-done | bytes 65568 | tf_op jit(solution)/shard_map/ppermute | solution.py:19
  119.6 1.6 %collective-permute-start.8 = (f32[128,128]{0,1:T(8,128)S(1)}, f32[128,128]{0,1:T(8,128)S(1)}, u32[]{:S(2)}, u32[]{:S(2)}) collective-permute-start(f32[128,128]{0,1:T(8,128)S(1)} %add.58), channel_id=1, source_target_pairs={{0,1},{1,0},{2,3},{3,2},{4,5},{5,4},{6,7},{7,6},{8,9},{9,8},{10,11... | collective-permute-start | bytes 196616 | tf_op jit(solution)/shard_map/ppermute | solution.py:19
  121.2 2.7 %collective-permute-done.8 = f32[128,128]{0,1:T(8,128)S(1)} collective-permute-done((f32[128,128]{0,1:T(8,128)S(1)}, f32[128,128]{0,1:T(8,128)S(1)}, u32[]{:S(2)}, u32[]{:S(2)}) %collective-permute-start.8) | collective-permute-done | bytes 65568 | tf_op jit(solution)/shard_map/ppermute | solution.py:19
  124.0 0.7 collective-permute-start.9
  124.7 3.6 %collective-permute-done.9 = f32[128,128]{0,1:T(8,128)S(1)} collective-permute-done((f32[128,128]{0,1:T(8,128)S(1)}, f32[128,128]{0,1:T(8,128)S(1)}, u32[]{:S(2)}, u32[]{:S(2)}) %collective-permute-start.9) | collective-permute-done | bytes 65568 | tf_op jit(solution)/shard_map/ppermute | solution.py:19
  128.3 2.4 %collective-permute-start.10 = (f32[128,128]{0,1:T(8,128)S(1)}, f32[128,128]{0,1:T(8,128)S(1)}, u32[]{:S(2)}, u32[]{:S(2)}) collective-permute-start(f32[128,128]{0,1:T(8,128)S(1)} %add.60), channel_id=1, source_target_pairs={{0,4},{1,5},{2,6},{3,7},{4,0},{5,1},{6,2},{7,3},{8,12},{9,13},{10,... | collective-permute-start | bytes 196616 | tf_op jit(solution)/shard_map/ppermute | solution.py:19
  130.8 4.4 %reshape.33 = f32[32,16,512]{2,1,0:T(8,128)} reshape(f32[8192,32]{1,0:T(8,128)} %copy.41) | data formatting | bytes 2097152 | tf_op jit(solution)/shard_map/reshape | solution.py:79
  135.3 11.7 %cholesky.45 = f32[128,128]{1,0:T(8,128)S(1)} custom-call(f32[128,128]{1,0:T(8,128)S(1)} %fusion.1), custom_call_target="Cholesky" | custom-call | tf_op jit(solution)/shard_map/jit(cholesky)/cholesky | solution.py:86
  147.7 0.7 multiply_bitcast_fusion
  148.3 0.7 copy.47
  (70 shorter events, 8.8 us)
Async XLA Ops:
  0.6 37.4 %copy-start = (f32[256,32]{0,1:T(8,128)S(1)}, f32[256,32]{0,1:T(8,128)}, u32[]{:S(2)}) copy-start(f32[256,32]{0,1:T(8,128)} %param.6) | copy-start | bytes 98308
  12.5 1.5 %collective-permute-start = (f32[192,128]{1,0:T(8,128)S(1)}, f32[192,128]{1,0:T(8,128)S(1)}, u32[]{:S(2)}, u32[]{:S(2)}) collective-permute-start(f32[192,128]{1,0:T(8,128)S(1)} %fusion), channel_id=1, source_target_pairs={{0,8},{8,0},{16,24},{24,16},{1,9},{9,1},{17,25},{25,17},{2,10},{10... | collective-permute-start | bytes 294920 | tf_op jit(solution)/shard_map/ppermute | solution.py:19
  14.0 6.0 %collective-permute-start.1 = (f32[192,128]{1,0:T(8,128)S(1)}, f32[192,128]{1,0:T(8,128)S(1)}, u32[]{:S(2)}, u32[]{:S(2)}) collective-permute-start(f32[192,128]{1,0:T(8,128)S(1)} %select_add_fusion), channel_id=1, source_target_pairs={{0,16},{8,24},{16,0},{24,8},{1,17},{9,25},{17,1},{25,9},{2,18},{10... | collective-permute-start | bytes 294920 | tf_op jit(solution)/shard_map/ppermute | solution.py:19
  20.0 4.7 %collective-permute-start.2 = (f32[192,128]{1,0:T(8,128)S(1)}, f32[192,128]{1,0:T(8,128)S(1)}, u32[]{:S(2)}, u32[]{:S(2)}) collective-permute-start(f32[192,128]{1,0:T(8,128)S(1)} %add.53), channel_id=1, source_target_pairs={{0,1},{1,0},{2,3},{3,2},{4,5},{5,4},{6,7},{7,6},{8,9},{9,8},{10,11... | collective-permute-start | bytes 294920 | tf_op jit(solution)/shard_map/ppermute | solution.py:19
  24.7 4.7 %collective-permute-start.3 = (f32[192,128]{1,0:T(8,128)S(1)}, f32[192,128]{1,0:T(8,128)S(1)}, u32[]{:S(2)}, u32[]{:S(2)}) collective-permute-start(f32[192,128]{1,0:T(8,128)S(1)} %add.54), channel_id=1, source_target_pairs={{0,2},{1,3},{2,0},{3,1},{4,6},{5,7},{6,4},{7,5},{8,10},{9,11},{10,... | collective-permute-start | bytes 294920 | tf_op jit(solution)/shard_map/ppermute | solution.py:19
  29.4 7.0 %collective-permute-start.4 = (f32[192,128]{1,0:T(8,128)S(1)}, f32[192,128]{1,0:T(8,128)S(1)}, u32[]{:S(2)}, u32[]{:S(2)}) collective-permute-start(f32[192,128]{1,0:T(8,128)S(1)} %add.55), channel_id=1, source_target_pairs={{0,4},{1,5},{2,6},{3,7},{4,0},{5,1},{6,2},{7,3},{8,12},{9,13},{10,... | collective-permute-start | bytes 294920 | tf_op jit(solution)/shard_map/ppermute | solution.py:19
  36.4 1.4 collective-permute-start.5
  82.2 13.5 %copy-start.1 = (f32[256,32]{0,1:T(8,128)}, f32[256,32]{0,1:T(8,128)S(1)}, u32[]{:S(2)}) copy-start(f32[256,32]{0,1:T(8,128)S(1)} %convolution_bitcast_fusion.2) | copy-start | bytes 98308
  114.0 1.3 collective-permute-start.6
  115.3 4.3 %collective-permute-start.7 = (f32[128,128]{0,1:T(8,128)S(1)}, f32[128,128]{0,1:T(8,128)S(1)}, u32[]{:S(2)}, u32[]{:S(2)}) collective-permute-start(f32[128,128]{0,1:T(8,128)S(1)} %add.57), channel_id=1, source_target_pairs={{0,16},{8,24},{16,0},{24,8},{1,17},{9,25},{17,1},{25,9},{2,18},{10... | collective-permute-start | bytes 196616 | tf_op jit(solution)/shard_map/ppermute | solution.py:19
  119.6 4.3 %collective-permute-start.8 = (f32[128,128]{0,1:T(8,128)S(1)}, f32[128,128]{0,1:T(8,128)S(1)}, u32[]{:S(2)}, u32[]{:S(2)}) collective-permute-start(f32[128,128]{0,1:T(8,128)S(1)} %add.58), channel_id=1, source_target_pairs={{0,1},{1,0},{2,3},{3,2},{4,5},{5,4},{6,7},{7,6},{8,9},{9,8},{10,11... | collective-permute-start | bytes 196616 | tf_op jit(solution)/shard_map/ppermute | solution.py:19
  124.0 4.3 %collective-permute-start.9 = (f32[128,128]{0,1:T(8,128)S(1)}, f32[128,128]{0,1:T(8,128)S(1)}, u32[]{:S(2)}, u32[]{:S(2)}) collective-permute-start(f32[128,128]{0,1:T(8,128)S(1)} %add.59), channel_id=1, source_target_pairs={{0,2},{1,3},{2,0},{3,1},{4,6},{5,7},{6,4},{7,5},{8,10},{9,11},{10,... | collective-permute-start | bytes 196616 | tf_op jit(solution)/shard_map/ppermute | solution.py:19
  128.3 6.8 %collective-permute-start.10 = (f32[128,128]{0,1:T(8,128)S(1)}, f32[128,128]{0,1:T(8,128)S(1)}, u32[]{:S(2)}, u32[]{:S(2)}) collective-permute-start(f32[128,128]{0,1:T(8,128)S(1)} %add.60), channel_id=1, source_target_pairs={{0,4},{1,5},{2,6},{3,7},{4,0},{5,1},{6,2},{7,3},{8,12},{9,13},{10,... | collective-permute-start | bytes 196616 | tf_op jit(solution)/shard_map/ppermute | solution.py:19

commit v2 on v0

v2 whole, which is shorter than its diff:
```python
import functools

import jax
import jax.numpy as jnp
from jax import lax
from jax.experimental import pallas as pl
from jax.experimental.pallas import tpu as pltpu
from jax.sharding import PartitionSpec as P

ITERS = 3
F32, BF16 = jnp.float32, jnp.bfloat16
LANES, SUBLANES = 128, 8

precise = lax.Precision.HIGHEST
ROWS_BY_ROWS = (((1,), (1,)), ((), ()))
COLUMNS_BY_COLUMNS = (((0,), (0,)), ((), ()))
VMEM = pl.BlockSpec(memory_space=pltpu.VMEM)


def bits(size):
    return [1 << b for b in range(size.bit_length() - 1)]


def partner(value, axis, mask):
    return lax.ppermute(value, axis, [(i, i ^ mask) for i in range(lax.axis_size(axis))])


def summed(value, skip_core=False):
    for axis in ("gx", "gy"):
        for bit in bits(lax.axis_size(axis))[1 if skip_core and axis == "gx" else 0 :]:
            value = value + partner(value, axis, bit)
    return value


def in_two(value):
    high = value.astype(BF16)
    return high, (value - high.astype(F32)).astype(BF16)


def tiles(value):
    rows, columns = value.shape
    return [
        [value[r : r + SUBLANES, c : min(c + LANES, columns)] for c in range(0, columns, LANES)]
        for r in range(0, rows, SUBLANES)
    ]


def joined(groups):
    return jnp.concatenate([jnp.concatenate(group, axis=1) for group in groups], axis=0)


def eliminated(gram, extra):
    gram = [list(group) for group in gram]
    extra = [list(group) for group in extra]
    row_id = lax.broadcasted_iota(jnp.int32, (SUBLANES, LANES), 0)

    def row(tile, r):
        return jnp.broadcast_to(tile[r : r + 1, :], tile.shape)

    def column(tile, c):
        return jnp.broadcast_to(tile[:, c : c + 1], (SUBLANES, LANES))

    def less(tile, factor, other):
        return tile - factor[:, : tile.shape[1]] * other

    for g in range(len(gram)):
        at, first = divmod(g * SUBLANES, LANES)
        both = [gram[h] + extra[h] for h in range(len(gram))]
        rows = [[row(t, q) for t in both[g]] for q in range(SUBLANES)]
        block = [
            [column(rows[a][at], first + b) if b >= a else None for b in range(SUBLANES)] for a in range(SUBLANES)
        ]
        below = range(g + 1, len(gram))
        columns = {h: [column(gram[h][at], first + q) for q in range(SUBLANES)] for h in below}
        scales, inverses = [], []
        for q in range(SUBLANES):
            scales.append(lax.rsqrt(block[q][q]))
            inverses.append(scales[q] * scales[q])
            for b in range(q + 1, SUBLANES):
                factor = block[q][b] * inverses[q]
                for c in range(b, SUBLANES):
                    block[b][c] = block[b][c] - factor * block[q][c]
                rows[b] = [less(t, factor, r) for t, r in zip(rows[b], rows[q])]
                for h in below:
                    columns[h][b] = columns[h][b] - factor * columns[h][q]
        for h in below:
            for q in range(SUBLANES):
                factor = columns[h][q] * inverses[q]
                both[h] = [less(t, factor, r) for t, r in zip(both[h], rows[q])]
        for q in range(SUBLANES):
            both[g] = [
                jnp.where((row_id == q)[:, : t.shape[1]], r * scales[q][:, : t.shape[1]], t)
                for t, r in zip(both[g], rows[q])
            ]
        for h in range(g, len(gram)):
            gram[h], extra[h] = both[h][: len(gram[h])], both[h][len(gram[h]) :]
    return gram, extra


def orthonormal(rows):
    for repeat in range(2):
        inner_gram = lax.dot_general(rows, rows, ROWS_BY_ROWS, precision=precise, preferred_element_type=F32)
        rows = joined(eliminated(tiles(inner_gram), tiles(rows))[1])
    return rows


def gram_kernel(field, out, square, cross):
    step = pl.program_id(0)
    high, low = in_two(field[...])
    new_square = lax.dot_general(high, high, COLUMNS_BY_COLUMNS, preferred_element_type=F32)
    new_cross = lax.dot_general(high, low, COLUMNS_BY_COLUMNS, preferred_element_type=F32)

    @pl.when(step == 0)
    def _():
        square[...] = new_square
        cross[...] = new_cross

    @pl.when(step > 0)
    def _():
        square[...] += new_square
        cross[...] += new_cross

    @pl.when(step == pl.num_programs(0) - 1)
    def _():
        half = square.shape[0] // 2
        quarter = half // 2
        full = square[...] + (cross[...] + cross[...].T)
        out[0, :half] = full[:half, :half]
        out[0, half:] = full[:quarter, half:]
        out[1, :half] = full[half:, half:]
        out[1, half:] = full[quarter:half, half:]


def local_gram(unfolded):
    rows, z = unfolded.shape
    block = rows // 2
    out = (2, z // 2 + z // 4, z // 2)
    return pl.pallas_call(
        gram_kernel,
        grid=(rows // block,),
        out_shape=jax.ShapeDtypeStruct(out, F32),
        in_specs=[pl.BlockSpec((block, z), lambda i: (i, 0))],
        out_specs=pl.BlockSpec(out, lambda i: (0, 0, 0)),
        scratch_shapes=[pltpu.VMEM((z, z), F32)] * 2,
        name="gram",
    )(unfolded)


def iterate_kernel(first, second, start, out, gram):
    half = gram.shape[0] // 2
    gram[:half, :half] = first[:half]
    gram[half:, half:] = second[:half]
    corner = jnp.concatenate([first[half:], second[half:]], axis=0)
    gram[:half, half:] = corner
    gram[half:, :half] = corner.T
    out[...] = start[...]

    @pl.loop(0, ITERS)
    def _(iteration):
        out[...] = orthonormal(jnp.dot(out[...], gram[...], precision=precise, preferred_element_type=F32))


def iterate(first, second, start_rows):
    z = start_rows.shape[1]
    return pl.pallas_call(
        iterate_kernel,
        out_shape=jax.ShapeDtypeStruct(start_rows.shape, F32),
        in_specs=[VMEM] * 3,
        out_specs=VMEM,
        scratch_shapes=[pltpu.VMEM((z, z), F32)],
        name="iterate",
    )(first, second, start_rows)


def core_kernel(species, y_cells, left, right, basis, core, by_y, weights, strip):
    rank, z = basis.shape
    cells = left.shape[0] // species
    pack = LANES // rank

    @pl.when(pl.program_id(0) == 0)
    def _():
        weights[...] = jnp.zeros_like(weights)
        for part, value in enumerate(in_two(basis[...])):
            for q in range(pack):
                weights[part * LANES + q * rank : part * LANES + (q + 1) * rank, q * z : (q + 1) * z] = value

    for t in range(species // pack):
        highs, lows = [], []
        for q in range(pack):
            for ref in (left, right):
                high, low = in_two(ref[pl.ds(t * pack + q, cells, stride=species), :])
                highs.append(high)
                lows.append(low)
        a = lax.dot_general(
            jnp.concatenate(highs, axis=1), weights[...], ROWS_BY_ROWS, preferred_element_type=F32
        )
        b = lax.dot_general(
            jnp.concatenate(lows, axis=1), weights[:LANES], ROWS_BY_ROWS, preferred_element_type=F32
        )
        strip[...] = (a[:, :LANES] + a[:, LANES:]) + b
        core[:, t * LANES : (t + 1) * LANES] = strip[...]
        for y in range(y_cells):
            by_y[y, :, t * LANES : (t + 1) * LANES] = strip[pl.ds(y, cells // y_cells, stride=y_cells), :]


def contract(unfolded, basis_rows, x_cells, y_cells, species):
    rows, z = unfolded.shape
    rank = basis_rows.shape[0]
    pack = LANES // rank
    steps = 2
    block, cells = rows // steps, rows // species // steps
    width = species * rank
    return pl.pallas_call(
        functools.partial(core_kernel, species, y_cells),
        grid=(steps,),
        out_shape=[
            jax.ShapeDtypeStruct((rows // species, width), F32),
            jax.ShapeDtypeStruct((y_cells, x_cells, width), F32),
        ],
        in_specs=[
            pl.BlockSpec((block, z // 2), lambda i: (i, 0)),
            pl.BlockSpec((block, z // 2), lambda i: (i, 1)),
            pl.BlockSpec((rank, z), lambda i: (0, 0)),
        ],
        out_specs=[
            pl.BlockSpec((cells, width), lambda i: (i, 0)),
            pl.BlockSpec((y_cells, x_cells // steps, width), lambda i: (0, i, 0)),
        ],
        scratch_shapes=[pltpu.VMEM((2 * LANES, pack * z), BF16), pltpu.VMEM((cells, LANES), F32)],
        name="core",
    )(unfolded, unfolded, basis_rows)


def product_kernel(place, *refs):
    pieces, out = refs[:-1], refs[-1]
    square = cross = 0.0
    for y in range(pieces[0].shape[0]):
        high, low = in_two(jnp.concatenate([piece[y] for piece in pieces], axis=0))
        square = square + lax.dot_general(high, high, ROWS_BY_ROWS, preferred_element_type=F32)
        cross = cross + lax.dot_general(high, low, ROWS_BY_ROWS, preferred_element_type=F32)
    total = square + (cross + cross.T)
    size = pieces[0].shape[1]
    for bit in bits(len(pieces)):
        step = size * bit
        swap = place[0] & bit != 0
        for axis in (0, 1):
            cuts = [lax.slice_in_dim(total, c, c + step, axis=axis) for c in range(0, total.shape[axis], step)]
            turned = jnp.concatenate([cuts[c ^ 1] for c in range(len(cuts))], axis=axis)
            total = jnp.where(swap, turned, total)
    out[...] = total


def product(place, pieces):
    n = len(pieces) * pieces[0].shape[1]
    return pl.pallas_call(
        product_kernel,
        out_shape=jax.ShapeDtypeStruct((n, n), F32),
        in_specs=[pl.BlockSpec(memory_space=pltpu.SMEM)] + [VMEM] * len(pieces),
        out_specs=VMEM,
        name="product",
    )(place, *pieces)


def triangle_kernel(scale, gram, out):
    upper = joined(eliminated(tiles(gram[...]), [[] for _ in range(0, gram.shape[0], SUBLANES)])[0])
    rows = lax.broadcasted_iota(jnp.int32, upper.shape, 0)
    columns = lax.broadcasted_iota(jnp.int32, upper.shape, 1)
    out[...] = jnp.where(columns >= rows, upper * scale, 0.0)


def triangle(gram, scale):
    return pl.pallas_call(
        functools.partial(triangle_kernel, scale),
        out_shape=jax.ShapeDtypeStruct(gram.shape, F32),
        in_specs=[VMEM],
        out_specs=VMEM,
        name="triangle",
    )(gram)


def local(state_field, start_basis):
    x_cells, y_cells, species, z_cells = state_field.shape
    rank_kept = start_basis.shape[1]
    unfolded = state_field.reshape(x_cells * y_cells * species, z_cells)
    halves = local_gram(unfolded)
    even = lax.axis_index("gx") % 2 == 0
    mine = jnp.where(even, halves[0], halves[1]) + partner(jnp.where(even, halves[1], halves[0]), "gx", 1)
    mine = summed(mine, skip_core=True)
    other = partner(mine, "gx", 1)
    basis_rows = iterate(jnp.where(even, mine, other), jnp.where(even, other, mine), start_basis.T)
    core_tensor, by_y = contract(unfolded, basis_rows, x_cells, y_cells, species)
    place, x_parts = lax.axis_index("gx"), lax.axis_size("gx")
    share = y_cells // x_parts
    pieces = []
    for d in range(x_parts):
        piece = lax.dynamic_slice_in_dim(by_y, (place ^ d) * share, share, axis=0)
        pieces.append(partner(piece, "gx", d) if d else piece)
    gram_x = summed(product(place.astype(jnp.int32).reshape(1), pieces))
    column_count = y_cells * lax.axis_size("gy") * species * rank_kept
    x_triangle = triangle(gram_x, 1.0 / column_count**0.5)
    return (core_tensor.reshape(x_cells, y_cells, species * rank_kept), basis_rows.T, x_triangle)


def solution(mesh):
    return jax.shard_map(
        local,
        mesh=mesh,
        in_specs=(P("gx", "gy", None, None), P()),
        out_specs=(P("gx", "gy", None), P(), P()),
        check_vma=False,
    )
```

time: 326 us -> 98.9 us (0.30)
  waiting for transfers between devices: 159 us -> 41 us
  other arithmetic: 53.2 us -> 4.16 us
  blocking collectives: 42.6 us -> 0 us
  matrix products: 38.3 us -> 0 us
  Pallas kernels: 0 us -> 31.1 us
  starting transfers between devices: 0.26 us -> 18.8 us
  local copies, waits for them, and re-layouts: 17.4 us -> 2.78 us
  between operations: 14.3 us -> 0.73 us
    psum x1 -> x0, waiting for transfers between devices: 129 us -> none  [local(): gram_z = lax.psum(local_gram, ('gx', 'gy'))]
    another operation x33 -> x0, other arithmetic: 52.5 us -> none  [the longest x18 21.6 us: orthonormal(): lower_factor = jnp.linalg.cholesky(inner_gram)]
    ppermute x0 -> x14, waiting for transfers between devices: none -> 41 us  [partner(): lax.ppermute(value, axis, [(i, i ^ mask) for i in range(lax.axis_size(axi...]
    psum x1 -> x0, blocking collectives: 37.1 us -> none  [local(): summed_row = lax.psum(product, 'gy')]
    dot_general x12 -> x0, matrix products: 36.8 us -> none  [the longest x1 17.8 us: local(): lax.dot_general(unfolded, unfolded, (((0,), (0,)), ((), ())), precision=p...]
    pallas_call x0 -> x5, Pallas kernels: none -> 31.1 us  [the longest x1 8.87 us: contract(): pl.pallas_call(functools.partial(core_kernel, species, y_cells), grid=(st...]
    all_gather x1 -> x0, waiting for transfers between devices: 30.1 us -> none  [local(): row_piece = lax.all_gather(core_tensor, 'gx', axis=0, tiled=True)]
    ppermute x0 -> x14, starting transfers between devices: none -> 18.8 us  [partner(): lax.ppermute(value, axis, [(i, i ^ mask) for i in range(lax.axis_size(axi...]
  transfers between devices with their start and end apart: 2 -> 14, of which waited for: 2 -> 13; matrix products, arithmetic and copies ran while one was open for 1% -> 0% of each run, Pallas kernels for 0% -> 0%
where the time goes in v2:
time: 98.9 us; the launch traced here: 98.6 us
  waiting for transfers between devices  41 us (41%)
  Pallas kernels  31.1 us (31%)
  starting transfers between devices  18.8 us (19%)
  other arithmetic  4.16 us (4%)
  local copies, waits for them, and re-layouts  2.78 us (3%)
    ppermute x14, waiting for transfers between devices, partner(): lax.ppermute(value, axis, [(i, i ^ mask) for i in range(lax.axis_size(axi...  41 us
    ppermute x14, starting transfers between devices, partner(): lax.ppermute(value, axis, [(i, i ^ mask) for i in range(lax.axis_size(axi...  18.8 us
    pallas_call x1, Pallas kernels, contract(): pl.pallas_call(functools.partial(core_kernel, species, y_cells), grid=(st...  8.87 us
    pallas_call x1, Pallas kernels, iterate(): pl.pallas_call(iterate_kernel, out_shape=jax.ShapeDtypeStruct(start_rows....  8.57 us
    pallas_call x1, Pallas kernels, local_gram(): pl.pallas_call(gram_kernel, grid=(rows // block,), out_shape=jax.ShapeDty...  5.65 us
    pallas_call x1, Pallas kernels, triangle(): pl.pallas_call(functools.partial(triangle_kernel, scale), out_shape=jax.S...  5.52 us
    pallas_call x1, Pallas kernels, product(): pl.pallas_call(product_kernel, out_shape=jax.ShapeDtypeStruct((n, n), F32...  2.51 us
    dynamic_slice x1, local copies, waits for them, and re-layouts, local(): piece = lax.dynamic_slice_in_dim(by_y, (place ^ d) * share, share, axis=0)  2 us
  transfers between devices with their start and end apart: 14, of which 13 were waited for; matrix products, arithmetic and copies ran while one was open for 0% of the time, Pallas kernels for 0%

profile of v2, /device:TPU:0, one launch (start us, length us, event | category | flops | bytes accessed | tf_op | source)
XLA Modules:
  0.0 98.6 jit_solution(5428821649414659912)
XLA Ops:
  0.6 5.6 %gram.1 = f32[2,192,128]{2,1,0:T(8,128)} custom-call(f32[8192,256]{1,0:T(8,128)} %bitcast.9), custom_call_target="tpu_custom_call" | custom-call | tf_op jit(solution)/shard_map/gram/pallas_call | solution.py:138
  6.3 1.0 select_bitcast_fusion
  7.2 0.6 collective-permute-start
  7.8 0.9 collective-permute-done
  8.8 1.0 bitcast_add_fusion
  9.7 2.9 %collective-permute-start.1 = (f32[192,128]{1,0:T(8,128)S(1)}, f32[192,128]{1,0:T(8,128)S(1)}, u32[]{:S(2)}, u32[]{:S(2)}) collective-permute-start(f32[192,128]{1,0:T(8,128)S(1)} %bitcast_add_fusion), channel_id=1, source_target_pairs={{0,16},{8,24},{16,0},{24,8},{1,17},{9,25},{17,1},{25,9},{2,18},{10... | collective-permute-start | bytes 294920 | tf_op jit(solution)/shard_map/ppermute | solution.py:25
  12.6 3.1 %collective-permute-done.1 = f32[192,128]{1,0:T(8,128)S(1)} collective-permute-done((f32[192,128]{1,0:T(8,128)S(1)}, f32[192,128]{1,0:T(8,128)S(1)}, u32[]{:S(2)}, u32[]{:S(2)}) %collective-permute-start.1) | collective-permute-done | bytes 98336 | tf_op jit(solution)/shard_map/ppermute | solution.py:25
  15.7 1.8 %collective-permute-start.2 = (f32[192,128]{1,0:T(8,128)S(1)}, f32[192,128]{1,0:T(8,128)S(1)}, u32[]{:S(2)}, u32[]{:S(2)}) collective-permute-start(f32[192,128]{1,0:T(8,128)S(1)} %add.48), channel_id=1, source_target_pairs={{0,1},{1,0},{2,3},{3,2},{4,5},{5,4},{6,7},{7,6},{8,9},{9,8},{10,11... | collective-permute-start | bytes 294920 | tf_op jit(solution)/shard_map/ppermute | solution.py:25
  17.6 2.8 %collective-permute-done.2 = f32[192,128]{1,0:T(8,128)S(1)} collective-permute-done((f32[192,128]{1,0:T(8,128)S(1)}, f32[192,128]{1,0:T(8,128)S(1)}, u32[]{:S(2)}, u32[]{:S(2)}) %collective-permute-start.2) | collective-permute-done | bytes 98336 | tf_op jit(solution)/shard_map/ppermute | solution.py:25
  20.4 1.9 %collective-permute-start.3 = (f32[192,128]{1,0:T(8,128)S(1)}, f32[192,128]{1,0:T(8,128)S(1)}, u32[]{:S(2)}, u32[]{:S(2)}) collective-permute-start(f32[192,128]{1,0:T(8,128)S(1)} %add.49), channel_id=1, source_target_pairs={{0,2},{1,3},{2,0},{3,1},{4,6},{5,7},{6,4},{7,5},{8,10},{9,11},{10,... | collective-permute-start | bytes 294920 | tf_op jit(solution)/shard_map/ppermute | solution.py:25
  22.3 2.8 %collective-permute-done.3 = f32[192,128]{1,0:T(8,128)S(1)} collective-permute-done((f32[192,128]{1,0:T(8,128)S(1)}, f32[192,128]{1,0:T(8,128)S(1)}, u32[]{:S(2)}, u32[]{:S(2)}) %collective-permute-start.3) | collective-permute-done | bytes 98336 | tf_op jit(solution)/shard_map/ppermute | solution.py:25
  25.1 3.3 %collective-permute-start.4 = (f32[192,128]{1,0:T(8,128)S(1)}, f32[192,128]{1,0:T(8,128)S(1)}, u32[]{:S(2)}, u32[]{:S(2)}) collective-permute-start(f32[192,128]{1,0:T(8,128)S(1)} %add.50), channel_id=1, source_target_pairs={{0,4},{1,5},{2,6},{3,7},{4,0},{5,1},{6,2},{7,3},{8,12},{9,13},{10,... | collective-permute-start | bytes 294920 | tf_op jit(solution)/shard_map/ppermute | solution.py:25
  28.5 3.6 %collective-permute-done.4 = f32[192,128]{1,0:T(8,128)S(1)} collective-permute-done((f32[192,128]{1,0:T(8,128)S(1)}, f32[192,128]{1,0:T(8,128)S(1)}, u32[]{:S(2)}, u32[]{:S(2)}) %collective-permute-start.4) | collective-permute-done | bytes 98336 | tf_op jit(solution)/shard_map/ppermute | solution.py:25
  32.1 0.1 collective-permute-start.5
  32.2 1.3 %collective-permute-done.5 = f32[192,128]{1,0:T(8,128)S(1)} collective-permute-done((f32[192,128]{1,0:T(8,128)S(1)}, f32[192,128]{1,0:T(8,128)S(1)}, u32[]{:S(2)}, u32[]{:S(2)}) %collective-permute-start.5) | collective-permute-done | bytes 98336 | tf_op jit(solution)/shard_map/ppermute | solution.py:25
  33.5 0.7 broadcast_select_fusion
  34.2 8.6 %iterate.1.basis = f32[32,256]{1,0:T(8,128)} custom-call(f32[192,128]{1,0:T(8,128)} %get-tuple-element.12.first, f32[192,128]{1,0:T(8,128)} %get-tuple-element.11.second, f32[32,256]{1,0:T(8,128)} %bitcast.13), custom_call_target="tpu_custom_call" | custom-call | tf_op jit(solution)/shard_map/iterate/pallas_call | solution.py:165
  42.8 8.9 %core.1 = (f32[512,512]{1,0:T(8,128)}, f32[16,32,512]{2,1,0:T(8,128)}) custom-call(f32[8192,256]{1,0:T(8,128)} %bitcast.10, f32[8192,256]{1,0:T(8,128)} %bitcast.11, f32[32,256]{1,0:T(8,128)} %iterate.1.basis), custom_call_target="tpu_custom_call" | custom-call | tf_op jit(solution)/shard_map/core/pallas_call | solution.py:213
  51.6 2.0 %constant_dynamic-slice_fusion = (f32[4,32,512]{2,1,0:T(8,128)S(1)}, f32[4,32,512]{2,1,0:T(8,128)S(1)}, f32[4,32,512]{2,1,0:T(8,128)S(1)}, f32[4,32,512]{2,1,0:T(8,128)}) fusion(f32[16,32,512]{2,1,0:T(8,128)} %get-tuple-element.6, s32[]{:T(128)S(6)} %select_n.59, s32[]{:T(128)S(6)} %select_n.58, s32[]{:T(128)S(6)} %select_n.57, s32[]{:T(128)S(6)} %select_n.56), kind=kLoop, calls=%fused_computation.4 | loop fusion | bytes 2097168 | tf_op jit(solution)/shard_map/dynamic_slice | solution.py:296
  53.6 1.2 %collective-permute-start.8 = (f32[4,32,512]{2,1,0:T(8,128)S(1)}, f32[4,32,512]{2,1,0:T(8,128)S(1)}, u32[]{:S(2)}, u32[]{:S(2)}) collective-permute-start(f32[4,32,512]{2,1,0:T(8,128)S(1)} %get-tuple-element.7), channel_id=1, source_target_pairs={{0,24},{8,16},{16,8},{24,0},{1,25},{9,17},{17,9},{25,1},{2,26},{10... | collective-permute-start | bytes 786440 | tf_op jit(solution)/shard_map/ppermute | solution.py:25
  54.9 0.5 collective-permute-start.7
  55.4 0.1 collective-permute-start.6
  55.5 6.4 %collective-permute-done.8.refs_3_ = f32[4,32,512]{2,1,0:T(8,128)S(1)} collective-permute-done((f32[4,32,512]{2,1,0:T(8,128)S(1)}, f32[4,32,512]{2,1,0:T(8,128)S(1)}, u32[]{:S(2)}, u32[]{:S(2)}) %collective-permute-start.8) | collective-permute-done | bytes 262176 | tf_op jit(solution)/shard_map/ppermute | solution.py:25
  61.9 0.0 copy-start
  61.9 6.0 %collective-permute-done.7.refs_2_ = f32[4,32,512]{2,1,0:T(8,128)S(1)} collective-permute-done((f32[4,32,512]{2,1,0:T(8,128)S(1)}, f32[4,32,512]{2,1,0:T(8,128)S(1)}, u32[]{:S(2)}, u32[]{:S(2)}) %collective-permute-start.7) | collective-permute-done | bytes 262176 | tf_op jit(solution)/shard_map/ppermute | solution.py:25
  67.8 0.0 copy-start.1
  67.9 0.0 collective-permute-done.6.refs_1_
  67.9 0.0 copy-start.2
  67.9 0.0 copy-done
  67.9 0.7 copy-done.1
  68.5 0.1 copy-done.2
  68.6 2.5 %product.1 = f32[128,128]{1,0:T(8,128)} custom-call(s32[1]{0:T(128)} %bitcast.6.place, f32[4,32,512]{2,1,0:T(8,128)} %get-tuple-element.10.refs_0_, f32[4,32,512]{2,1,0:T(8,128)} %copy-done.2, f32[4,32,512]{2,1,0:T(8,128)} %copy-done.1, f32[4,32,512]{2,1,0:T(8,128)} %copy-done), custom_call_target="tpu_custom_call" | custom-call | tf_op jit(solution)/shard_map/product/pallas_call | solution.py:255
  71.1 0.0 collective-permute-start.9
  71.2 1.5 %collective-permute-done.9 = f32[128,128]{1,0:T(8,128)S(1)} collective-permute-done((f32[128,128]{1,0:T(8,128)}, f32[128,128]{1,0:T(8,128)S(1)}, u32[]{:S(2)}, u32[]{:S(2)}) %collective-permute-start.9) | collective-permute-done | bytes 65568 | tf_op jit(solution)/shard_map/ppermute | solution.py:25
  72.6 0.9 add.56
  73.5 1.6 %collective-permute-start.10 = (f32[128,128]{1,0:T(8,128)S(1)}, f32[128,128]{1,0:T(8,128)S(1)}, u32[]{:S(2)}, u32[]{:S(2)}) collective-permute-start(f32[128,128]{1,0:T(8,128)S(1)} %add.56), channel_id=1, source_target_pairs={{0,16},{8,24},{16,0},{24,8},{1,17},{9,25},{17,1},{25,9},{2,18},{10... | collective-permute-start | bytes 196616 | tf_op jit(solution)/shard_map/ppermute | solution.py:25
  75.0 2.8 %collective-permute-done.10 = f32[128,128]{1,0:T(8,128)S(1)} collective-permute-done((f32[128,128]{1,0:T(8,128)S(1)}, f32[128,128]{1,0:T(8,128)S(1)}, u32[]{:S(2)}, u32[]{:S(2)}) %collective-permute-start.10) | collective-permute-done | bytes 65568 | tf_op jit(solution)/shard_map/ppermute | solution.py:25
  77.8 1.6 %collective-permute-start.11 = (f32[128,128]{1,0:T(8,128)S(1)}, f32[128,128]{1,0:T(8,128)S(1)}, u32[]{:S(2)}, u32[]{:S(2)}) collective-permute-start(f32[128,128]{1,0:T(8,128)S(1)} %add.57), channel_id=1, source_target_pairs={{0,1},{1,0},{2,3},{3,2},{4,5},{5,4},{6,7},{7,6},{8,9},{9,8},{10,11... | collective-permute-start | bytes 196616 | tf_op jit(solution)/shard_map/ppermute | solution.py:25
  79.4 2.7 %collective-permute-done.11 = f32[128,128]{1,0:T(8,128)S(1)} collective-permute-done((f32[128,128]{1,0:T(8,128)S(1)}, f32[128,128]{1,0:T(8,128)S(1)}, u32[]{:S(2)}, u32[]{:S(2)}) %collective-permute-start.11) | collective-permute-done | bytes 65568 | tf_op jit(solution)/shard_map/ppermute | solution.py:25
  82.1 0.7 collective-permute-start.12
  82.9 3.6 %collective-permute-done.12 = f32[128,128]{1,0:T(8,128)S(1)} collective-permute-done((f32[128,128]{1,0:T(8,128)S(1)}, f32[128,128]{1,0:T(8,128)S(1)}, u32[]{:S(2)}, u32[]{:S(2)}) %collective-permute-start.12) | collective-permute-done | bytes 65568 | tf_op jit(solution)/shard_map/ppermute | solution.py:25
  86.5 2.4 %collective-permute-start.13 = (f32[128,128]{1,0:T(8,128)S(1)}, f32[128,128]{1,0:T(8,128)S(1)}, u32[]{:S(2)}, u32[]{:S(2)}) collective-permute-start(f32[128,128]{1,0:T(8,128)S(1)} %add.59), channel_id=1, source_target_pairs={{0,4},{1,5},{2,6},{3,7},{4,0},{5,1},{6,2},{7,3},{8,12},{9,13},{10,... | collective-permute-start | bytes 196616 | tf_op jit(solution)/shard_map/ppermute | solution.py:25
  88.9 3.5 %collective-permute-done.13 = f32[128,128]{1,0:T(8,128)S(1)} collective-permute-done((f32[128,128]{1,0:T(8,128)S(1)}, f32[128,128]{1,0:T(8,128)S(1)}, u32[]{:S(2)}, u32[]{:S(2)}) %collective-permute-start.13) | collective-permute-done | bytes 65568 | tf_op jit(solution)/shard_map/ppermute | solution.py:25
  92.4 0.6 add.60.gram
  93.1 5.5 %triangle.1 = f32[128,128]{1,0:T(8,128)} custom-call(f32[128,128]{1,0:T(8,128)} %add.60.gram), custom_call_target="tpu_custom_call" | custom-call | tf_op jit(solution)/shard_map/triangle/pallas_call | solution.py:272
  (7 shorter events, 0.1 us)
Async XLA Ops:
  7.2 1.5 %collective-permute-start = (f32[192,128]{1,0:T(8,128)S(1)}, f32[192,128]{1,0:T(8,128)S(1)}, u32[]{:S(2)}, u32[]{:S(2)}) collective-permute-start(f32[192,128]{1,0:T(8,128)S(1)} %select_bitcast_fusion), channel_id=1, source_target_pairs={{0,8},{8,0},{16,24},{24,16},{1,9},{9,1},{17,25},{25,17},{2,10},{10... | collective-permute-start | bytes 294920 | tf_op jit(solution)/shard_map/ppermute | solution.py:25
  9.7 6.0 %collective-permute-start.1 = (f32[192,128]{1,0:T(8,128)S(1)}, f32[192,128]{1,0:T(8,128)S(1)}, u32[]{:S(2)}, u32[]{:S(2)}) collective-permute-start(f32[192,128]{1,0:T(8,128)S(1)} %bitcast_add_fusion), channel_id=1, source_target_pairs={{0,16},{8,24},{16,0},{24,8},{1,17},{9,25},{17,1},{25,9},{2,18},{10... | collective-permute-start | bytes 294920 | tf_op jit(solution)/shard_map/ppermute | solution.py:25
  15.7 4.7 %collective-permute-start.2 = (f32[192,128]{1,0:T(8,128)S(1)}, f32[192,128]{1,0:T(8,128)S(1)}, u32[]{:S(2)}, u32[]{:S(2)}) collective-permute-start(f32[192,128]{1,0:T(8,128)S(1)} %add.48), channel_id=1, source_target_pairs={{0,1},{1,0},{2,3},{3,2},{4,5},{5,4},{6,7},{7,6},{8,9},{9,8},{10,11... | collective-permute-start | bytes 294920 | tf_op jit(solution)/shard_map/ppermute | solution.py:25
  20.4 4.7 %collective-permute-start.3 = (f32[192,128]{1,0:T(8,128)S(1)}, f32[192,128]{1,0:T(8,128)S(1)}, u32[]{:S(2)}, u32[]{:S(2)}) collective-permute-start(f32[192,128]{1,0:T(8,128)S(1)} %add.49), channel_id=1, source_target_pairs={{0,2},{1,3},{2,0},{3,1},{4,6},{5,7},{6,4},{7,5},{8,10},{9,11},{10,... | collective-permute-start | bytes 294920 | tf_op jit(solution)/shard_map/ppermute | solution.py:25
  25.1 7.0 %collective-permute-start.4 = (f32[192,128]{1,0:T(8,128)S(1)}, f32[192,128]{1,0:T(8,128)S(1)}, u32[]{:S(2)}, u32[]{:S(2)}) collective-permute-start(f32[192,128]{1,0:T(8,128)S(1)} %add.50), channel_id=1, source_target_pairs={{0,4},{1,5},{2,6},{3,7},{4,0},{5,1},{6,2},{7,3},{8,12},{9,13},{10,... | collective-permute-start | bytes 294920 | tf_op jit(solution)/shard_map/ppermute | solution.py:25
  32.1 1.4 %collective-permute-start.5 = (f32[192,128]{1,0:T(8,128)S(1)}, f32[192,128]{1,0:T(8,128)S(1)}, u32[]{:S(2)}, u32[]{:S(2)}) collective-permute-start(f32[192,128]{1,0:T(8,128)S(1)} %add.51), channel_id=1, source_target_pairs={{0,8},{8,0},{16,24},{24,16},{1,9},{9,1},{17,25},{25,17},{2,10},{10... | collective-permute-start | bytes 294920 | tf_op jit(solution)/shard_map/ppermute | solution.py:25
  53.6 8.3 %collective-permute-start.8 = (f32[4,32,512]{2,1,0:T(8,128)S(1)}, f32[4,32,512]{2,1,0:T(8,128)S(1)}, u32[]{:S(2)}, u32[]{:S(2)}) collective-permute-start(f32[4,32,512]{2,1,0:T(8,128)S(1)} %get-tuple-element.7), channel_id=1, source_target_pairs={{0,24},{8,16},{16,8},{24,0},{1,25},{9,17},{17,9},{25,1},{2,26},{10... | collective-permute-start | bytes 786440 | tf_op jit(solution)/shard_map/ppermute | solution.py:25
  54.9 13.0 %collective-permute-start.7 = (f32[4,32,512]{2,1,0:T(8,128)S(1)}, f32[4,32,512]{2,1,0:T(8,128)S(1)}, u32[]{:S(2)}, u32[]{:S(2)}) collective-permute-start(f32[4,32,512]{2,1,0:T(8,128)S(1)} %get-tuple-element.8), channel_id=1, source_target_pairs={{0,16},{8,24},{16,0},{24,8},{1,17},{9,25},{17,1},{25,9},{2,18},{10... | collective-permute-start | bytes 786440 | tf_op jit(solution)/shard_map/ppermute | solution.py:25
  55.4 12.4 %collective-permute-start.6 = (f32[4,32,512]{2,1,0:T(8,128)S(1)}, f32[4,32,512]{2,1,0:T(8,128)S(1)}, u32[]{:S(2)}, u32[]{:S(2)}) collective-permute-start(f32[4,32,512]{2,1,0:T(8,128)S(1)} %get-tuple-element.9), channel_id=1, source_target_pairs={{0,8},{8,0},{16,24},{24,16},{1,9},{9,1},{17,25},{25,17},{2,10},{10... | collective-permute-start | bytes 786440 | tf_op jit(solution)/shard_map/ppermute | solution.py:25
  61.9 6.0 %copy-start = (f32[4,32,512]{2,1,0:T(8,128)}, f32[4,32,512]{2,1,0:T(8,128)S(1)}, u32[]{:S(2)}) copy-start(f32[4,32,512]{2,1,0:T(8,128)S(1)} %collective-permute-done.8.refs_3_) | copy-start | bytes 786436
  67.8 0.7 copy-start.1
  67.9 0.8 copy-start.2
  71.1 1.5 %collective-permute-start.9 = (f32[128,128]{1,0:T(8,128)}, f32[128,128]{1,0:T(8,128)S(1)}, u32[]{:S(2)}, u32[]{:S(2)}) collective-permute-start(f32[128,128]{1,0:T(8,128)} %product.1), channel_id=1, source_target_pairs={{0,8},{8,0},{16,24},{24,16},{1,9},{9,1},{17,25},{25,17},{2,10},{10... | collective-permute-start | bytes 196616 | tf_op jit(solution)/shard_map/ppermute | solution.py:25
  73.5 4.3 %collective-permute-start.10 = (f32[128,128]{1,0:T(8,128)S(1)}, f32[128,128]{1,0:T(8,128)S(1)}, u32[]{:S(2)}, u32[]{:S(2)}) collective-permute-start(f32[128,128]{1,0:T(8,128)S(1)} %add.56), channel_id=1, source_target_pairs={{0,16},{8,24},{16,0},{24,8},{1,17},{9,25},{17,1},{25,9},{2,18},{10... | collective-permute-start | bytes 196616 | tf_op jit(solution)/shard_map/ppermute | solution.py:25
  77.8 4.3 %collective-permute-start.11 = (f32[128,128]{1,0:T(8,128)S(1)}, f32[128,128]{1,0:T(8,128)S(1)}, u32[]{:S(2)}, u32[]{:S(2)}) collective-permute-start(f32[128,128]{1,0:T(8,128)S(1)} %add.57), channel_id=1, source_target_pairs={{0,1},{1,0},{2,3},{3,2},{4,5},{5,4},{6,7},{7,6},{8,9},{9,8},{10,11... | collective-permute-start | bytes 196616 | tf_op jit(solution)/shard_map/ppermute | solution.py:25
  82.1 4.3 %collective-permute-start.12 = (f32[128,128]{1,0:T(8,128)S(1)}, f32[128,128]{1,0:T(8,128)S(1)}, u32[]{:S(2)}, u32[]{:S(2)}) collective-permute-start(f32[128,128]{1,0:T(8,128)S(1)} %add.58), channel_id=1, source_target_pairs={{0,2},{1,3},{2,0},{3,1},{4,6},{5,7},{6,4},{7,5},{8,10},{9,11},{10,... | collective-permute-start | bytes 196616 | tf_op jit(solution)/shard_map/ppermute | solution.py:25
  86.5 5.9 %collective-permute-start.13 = (f32[128,128]{1,0:T(8,128)S(1)}, f32[128,128]{1,0:T(8,128)S(1)}, u32[]{:S(2)}, u32[]{:S(2)}) collective-permute-start(f32[128,128]{1,0:T(8,128)S(1)} %add.59), channel_id=1, source_target_pairs={{0,4},{1,5},{2,6},{3,7},{4,0},{5,1},{6,2},{7,3},{8,12},{9,13},{10,... | collective-permute-start | bytes 196616 | tf_op jit(solution)/shard_map/ppermute | solution.py:25

commit v3 on v2

v3 whole, which is shorter than its diff:
```python
import functools

import jax
import jax.numpy as jnp
from jax import lax
from jax.experimental import pallas as pl
from jax.experimental.pallas import tpu as pltpu
from jax.sharding import PartitionSpec as P

ITERS = 3
F32, BF16 = jnp.float32, jnp.bfloat16
LANES, SUBLANES = 128, 8

precise = lax.Precision.HIGHEST
ROWS_BY_ROWS = (((1,), (1,)), ((), ()))
COLUMNS_BY_COLUMNS = (((0,), (0,)), ((), ()))
VMEM = pl.BlockSpec(memory_space=pltpu.VMEM)
SMEM = pl.BlockSpec(memory_space=pltpu.SMEM)
HBM = pl.BlockSpec(memory_space=pltpu.HBM)
SMALL = pltpu.CompilerParams(vmem_limit_bytes=32 << 20)


def bits(size):
    return [1 << b for b in range(size.bit_length() - 1)]


def partner(value, axis, mask):
    return lax.ppermute(value, axis, [(i, i ^ mask) for i in range(lax.axis_size(axis))])


def summed(value, skip_core=False):
    for axis in ("gx", "gy"):
        for bit in bits(lax.axis_size(axis))[1 if skip_core and axis == "gx" else 0 :]:
            value = value + partner(value, axis, bit)
    return value


def in_two(value):
    high = value.astype(BF16)
    return high, (value - high.astype(F32)).astype(BF16)


def tiles(value):
    rows, columns = value.shape
    return [
        [value[r : r + SUBLANES, c : min(c + LANES, columns)] for c in range(0, columns, LANES)]
        for r in range(0, rows, SUBLANES)
    ]


def joined(groups):
    return jnp.concatenate([jnp.concatenate(group, axis=1) for group in groups], axis=0)


def eliminated(gram, extra):
    gram = [list(group) for group in gram]
    extra = [list(group) for group in extra]
    row_id = lax.broadcasted_iota(jnp.int32, (SUBLANES, LANES), 0)

    def row(tile, r):
        return jnp.broadcast_to(tile[r : r + 1, :], tile.shape)

    def column(tile, c):
        return jnp.broadcast_to(tile[:, c : c + 1], (SUBLANES, LANES))

    def less(tile, factor, other):
        return tile - factor[:, : tile.shape[1]] * other

    for g in range(len(gram)):
        at, first = divmod(g * SUBLANES, LANES)
        both = [gram[h] + extra[h] for h in range(len(gram))]
        rows = [[row(t, q) for t in both[g]] for q in range(SUBLANES)]
        block = [
            [column(rows[a][at], first + b) if b >= a else None for b in range(SUBLANES)] for a in range(SUBLANES)
        ]
        below = range(g + 1, len(gram))
        columns = {h: [column(gram[h][at], first + q) for q in range(SUBLANES)] for h in below}
        scales, inverses = [], []
        for q in range(SUBLANES):
            scales.append(lax.rsqrt(block[q][q]))
            inverses.append(scales[q] * scales[q])
            for b in range(q + 1, SUBLANES):
                factor = block[q][b] * inverses[q]
                for c in range(b, SUBLANES):
                    block[b][c] = block[b][c] - factor * block[q][c]
                rows[b] = [less(t, factor, r) for t, r in zip(rows[b], rows[q])]
                for h in below:
                    columns[h][b] = columns[h][b] - factor * columns[h][q]
        for h in below:
            for q in range(SUBLANES):
                factor = columns[h][q] * inverses[q]
                both[h] = [less(t, factor, r) for t, r in zip(both[h], rows[q])]
        for q in range(SUBLANES):
            both[g] = [
                jnp.where((row_id == q)[:, : t.shape[1]], r * scales[q][:, : t.shape[1]], t)
                for t, r in zip(both[g], rows[q])
            ]
        for h in range(g, len(gram)):
            gram[h], extra[h] = both[h][: len(gram[h])], both[h][len(gram[h]) :]
    return gram, extra


def orth_pass(rows, *more):
    inner_gram = lax.dot_general(rows, rows, ROWS_BY_ROWS, precision=precise, preferred_element_type=F32)
    widths = [v.shape[1] for v in (rows, *more)]
    extra = [sum(parts, []) for parts in zip(*(tiles(v) for v in (rows, *more)))]
    groups = eliminated(tiles(inner_gram), extra)[1]
    out, at = [], 0
    for width in widths:
        count = -(-width // LANES)
        out.append(joined([group[at : at + count] for group in groups]))
        at += count
    return out


def triangle_ids(n):
    return lax.broadcasted_iota(jnp.int32, (n, n), 0), lax.broadcasted_iota(jnp.int32, (n, n), 1)


def folded(full):
    half = full.shape[0] // 2
    r, c = triangle_ids(half)
    corner = full[half:, half:]
    diagonal = jnp.sum(jnp.where(r == c, corner, 0.0), axis=0, keepdims=True)
    return jnp.where(r > c, corner, full[:half, :half]), full[:half, half:], diagonal


def opened(fold, upper, diagonal):
    half = fold.shape[0]
    r, c = triangle_ids(half)
    turned = fold.T
    first = jnp.where(c >= r, fold, turned)
    second = jnp.where(r > c, fold, jnp.where(r == c, jnp.broadcast_to(diagonal, fold.shape), turned))
    return jnp.concatenate(
        [jnp.concatenate([first, upper], axis=1), jnp.concatenate([upper.T, second], axis=1)], axis=0
    )


def species_weights(rows, repeat):
    high, low = in_two(jnp.concatenate([rows] * repeat, axis=0).T)
    weights = jnp.concatenate([high, low], axis=1)
    return jnp.concatenate([weights, weights], axis=0)


def times(value, weights):
    out = jnp.dot(jnp.concatenate(in_two(value), axis=1), weights, preferred_element_type=F32)
    half = out.shape[1] // 2
    return out[:, :half] + out[:, half:]


def packed(narrow, first, count, stride, rank):
    lane = lax.broadcasted_iota(jnp.int32, (count, LANES), 1)
    pack = LANES // rank
    out = narrow[pl.ds(first + pack - 1, count, stride=stride), :]
    for q in range(pack - 2, -1, -1):
        out = jnp.where(lane < (q + 1) * rank, narrow[pl.ds(first + q, count, stride=stride), :], out)
    return out


def gram_kernel(cuts, place, field, mine, other, held, arrived):
    copies = [
        pltpu.make_async_copy(field.at[a:b], held.at[a:b], arrived.at[i])
        for i, (a, b) in enumerate(zip(cuts[:-1], cuts[1:]))
    ]
    for copy in copies:
        copy.start()
    square = cross = 0.0
    for copy, a, b in zip(copies, cuts[:-1], cuts[1:]):
        copy.wait()
        high, low = in_two(held[a:b])
        square = square + lax.dot_general(high, high, COLUMNS_BY_COLUMNS, preferred_element_type=F32)
        cross = cross + lax.dot_general(high, low, COLUMNS_BY_COLUMNS, preferred_element_type=F32)
    fold, upper, diagonal = folded(square + (cross + cross.T))
    half = fold.shape[0]
    edge = SUBLANES
    even = place[0] & 1 == 0

    def put(first, second):
        first[:half] = fold
        first[half:] = upper[:edge]
        second[: half - edge] = upper[edge:]
        second[half - edge :] = jnp.broadcast_to(diagonal, (2 * edge, half))

    @pl.when(even)
    def _():
        put(mine, other)

    @pl.when(jnp.logical_not(even))
    def _():
        put(other, mine)


def local_gram(place, unfolded):
    rows, z = unfolded.shape
    cuts = [0, rows // 8, rows // 2, rows]
    out = jax.ShapeDtypeStruct((z // 2 + SUBLANES, z // 2), F32)
    return pl.pallas_call(
        functools.partial(gram_kernel, cuts),
        out_shape=[out, out, jax.ShapeDtypeStruct((rows, z), F32)],
        in_specs=[SMEM, HBM],
        out_specs=[VMEM] * 3,
        scratch_shapes=[pltpu.SemaphoreType.DMA((len(cuts) - 1,))],
        compiler_params=pltpu.CompilerParams(vmem_limit_bytes=32 << 20),
        name="gram",
    )(place, unfolded)


def begin_kernel(place, mine, other, start, basis, image, gram):
    half = mine.shape[1]
    edge = SUBLANES
    even = place[0] & 1 == 0
    first = jnp.where(even, mine[...], other[...])
    second = jnp.where(even, other[...], mine[...])
    gram[...] = opened(
        first[:half],
        jnp.concatenate([first[half:], second[: half - edge]], axis=0),
        second[half - edge : half - edge + 1],
    )
    basis[...] = start[...]

    def multiplied():
        return jnp.dot(basis[...], gram[...], precision=precise, preferred_element_type=F32)

    @pl.loop(0, ITERS - 2)
    def _(iteration):
        basis[...] = orth_pass(*orth_pass(multiplied()))[0]

    basis[...] = orth_pass(multiplied())[0]
    image[...] = multiplied()


def begin(place, mine, other, start_rows):
    z = start_rows.shape[1]
    rows = jax.ShapeDtypeStruct(start_rows.shape, F32)
    return pl.pallas_call(
        begin_kernel,
        out_shape=[rows, rows, jax.ShapeDtypeStruct((z, z), F32)],
        in_specs=[SMEM] + [VMEM] * 3,
        out_specs=[VMEM] * 3,
        compiler_params=SMALL,
        name="begin",
    )(place, mine, other, start_rows)


def finish_kernel(basis, gram, out, factor):
    rank = basis.shape[0]
    r, c = triangle_ids(rank)
    rows, turn = orth_pass(basis[...], jnp.where(r == c, 1.0, 0.0))
    rows = jnp.dot(rows, gram[...], precision=precise, preferred_element_type=F32)
    for repeat in range(2):
        rows, turn = orth_pass(rows, turn)
    out[...] = rows
    factor[...] = turn


def finish(basis, gram):
    rank, z = basis.shape
    return pl.pallas_call(
        finish_kernel,
        out_shape=[jax.ShapeDtypeStruct((rank, z), F32), jax.ShapeDtypeStruct((rank, rank), F32)],
        in_specs=[VMEM] * 2,
        out_specs=[VMEM] * 2,
        compiler_params=SMALL,
        cost_estimate=pl.CostEstimate(flops=1 << 30, bytes_accessed=1 << 24, transcendentals=0),
        name="finish",
    )(basis, gram)


def ahead_kernel(chunks, species, place, field, image, *refs):
    outs, narrow = refs[:-1], refs[-1]
    half = len(outs)
    share, x_cells, width = outs[0].shape
    rank = image.shape[0]
    across = half * share * species
    far = 1 - place[0] // half
    start = pl.multiple_of(far * across, across)
    step = x_cells // chunks
    weights = species_weights(image[...], LANES // rank)
    for i in range(chunks):
        cells = field[i * step : (i + 1) * step, pl.ds(start, across), :]
        narrow[...] = times(cells.reshape(step * across, cells.shape[2]), weights)
        for d, out in enumerate(outs):
            place_of_d = (place[0] ^ d) & (half - 1)
            for y in range(share):
                first = pl.multiple_of((place_of_d * share + y) * species, species)
                for t in range(width // LANES):
                    out[y, i * step : (i + 1) * step, t * LANES : (t + 1) * LANES] = packed(
                        narrow, first + t * (LANES // rank), step, across, rank
                    )


def contract_ahead(place, field, image, x_cells, y_cells, species, x_parts):
    z = field.shape[1]
    rank = image.shape[0]
    chunks = 2
    across = y_cells // 2 * species
    piece = jax.ShapeDtypeStruct((y_cells // x_parts, x_cells, species * rank), F32)
    return pl.pallas_call(
        functools.partial(ahead_kernel, chunks, species),
        out_shape=[piece] * (x_parts // 2),
        in_specs=[SMEM, VMEM, VMEM],
        out_specs=[VMEM] * (x_parts // 2),
        scratch_shapes=[pltpu.VMEM((x_cells // chunks * across, LANES), F32)],
        compiler_params=SMALL,
        name="ahead",
    )(place, field.reshape(x_cells, y_cells * species, z), image)


def core_kernel(species, y_cells, place, field, basis, core, *refs):
    outs, (weights, narrow, strip) = refs[:-3], refs[-3:]
    share, step, width = outs[0].shape
    rank = basis.shape[0]
    cells = core.shape[0]
    half = len(outs)
    near = place[0] // half * half

    @pl.when(pl.program_id(0) == 0)
    def _():
        weights[...] = species_weights(basis[...], LANES // rank)

    block = narrow.shape[0]
    narrow[...] = times(field[pl.ds(pl.multiple_of(pl.program_id(0) * block, block), block), :], weights[...])
    for t in range(width // LANES):
        lanes = slice(t * LANES, (t + 1) * LANES)
        strip[...] = packed(narrow, t * (LANES // rank), cells, species, rank)
        core[:, lanes] = strip[...]
        for d, out in enumerate(outs):
            part = near + ((place[0] ^ d) & (half - 1))
            for y in range(share):
                out[y, :, lanes] = strip[pl.ds(part * share + y, step, stride=y_cells), :]


def contract(place, unfolded, basis, x_cells, y_cells, species, x_parts):
    rows, z = unfolded.shape
    rank = basis.shape[0]
    steps = 4
    block, cells = rows // steps, rows // species // steps
    width = species * rank
    share = y_cells // x_parts
    pieces = x_parts // 2
    return pl.pallas_call(
        functools.partial(core_kernel, species, y_cells),
        grid=(steps,),
        out_shape=[jax.ShapeDtypeStruct((rows // species, width), F32)]
        + [jax.ShapeDtypeStruct((share, x_cells, width), F32)] * pieces,
        in_specs=[
            SMEM,
            VMEM,
            pl.BlockSpec((rank, z), lambda i: (0, 0)),
        ],
        out_specs=[pl.BlockSpec((cells, width), lambda i: (i, 0))]
        + [pl.BlockSpec((share, x_cells // steps, width), lambda i: (0, i, 0))] * pieces,
        scratch_shapes=[
            pltpu.VMEM((2 * z, 2 * LANES), BF16),
            pltpu.VMEM((block, LANES), F32),
            pltpu.VMEM((cells, LANES), F32),
        ],
        compiler_params=SMALL,
        cost_estimate=pl.CostEstimate(flops=1 << 31, bytes_accessed=1 << 24, transcendentals=0),
        name="core",
    )(place, unfolded, basis)


def product_kernel(place, factor, *refs):
    pieces, (out, turn) = refs[:-2], refs[-2:]
    share, size, width = pieces[0].shape
    rank = factor.shape[0]
    near, far = pieces[: len(pieces) // 2], pieces[len(pieces) // 2 :]
    turn[...] = jnp.zeros_like(turn)
    for part, value in enumerate(in_two(factor[...])):
        for side in range(2):
            for q in range(LANES // rank):
                turn[
                    part * LANES + q * rank : part * LANES + (q + 1) * rank,
                    side * LANES + q * rank : side * LANES + (q + 1) * rank,
                ] = value
    strips = [
        piece[y, :, t : t + LANES] for piece in far for y in range(share) for t in range(0, width, LANES)
    ]
    both = jnp.concatenate(in_two(jnp.concatenate(strips, axis=0)), axis=1)
    turned = lax.dot_general(both, turn[...], ROWS_BY_ROWS, preferred_element_type=F32)
    turned = turned[:, :LANES] + turned[:, LANES:]
    count = width // LANES
    square = cross = 0.0
    for y in range(share):
        rows = [piece[y] for piece in near]
        for d in range(len(far)):
            at = (d * share + y) * count
            rows.append(
                jnp.concatenate([turned[(at + t) * size : (at + t + 1) * size] for t in range(count)], axis=1)
            )
        high, low = in_two(jnp.concatenate(rows, axis=0))
        square = square + lax.dot_general(high, high, ROWS_BY_ROWS, preferred_element_type=F32)
        cross = cross + lax.dot_general(high, low, ROWS_BY_ROWS, preferred_element_type=F32)
    total = square + (cross + cross.T)
    for bit in bits(len(pieces)):
        step = size * bit
        swap = place[0] & bit != 0
        for axis in (0, 1):
            parts = [lax.slice_in_dim(total, c, c + step, axis=axis) for c in range(0, total.shape[axis], step)]
            swapped = jnp.concatenate([parts[c ^ 1] for c in range(len(parts))], axis=axis)
            total = jnp.where(swap, swapped, total)
    fold, upper, diagonal = folded(total)
    half = fold.shape[0]
    out[:half] = jnp.concatenate([fold, upper], axis=1)
    out[half:] = jnp.broadcast_to(jnp.concatenate([diagonal, diagonal], axis=1), (SUBLANES, 2 * half))


def product(place, factor, pieces):
    n = len(pieces) * pieces[0].shape[1]
    return pl.pallas_call(
        product_kernel,
        out_shape=jax.ShapeDtypeStruct((n // 2 + SUBLANES, n), F32),
        in_specs=[SMEM] + [VMEM] * (len(pieces) + 1),
        out_specs=VMEM,
        scratch_shapes=[pltpu.VMEM((2 * LANES, 2 * LANES), BF16)],
        compiler_params=SMALL,
        name="product",
    )(place, factor, *pieces)


def triangle_kernel(scale, gram, out):
    half = gram.shape[1] // 2
    full = opened(gram[:half, :half], gram[:half, half:], gram[half : half + 1, :half])
    upper = joined(eliminated(tiles(full), [[] for _ in range(0, 2 * half, SUBLANES)])[0])
    r, c = triangle_ids(2 * half)
    out[...] = jnp.where(c >= r, upper * scale, 0.0)


def triangle(gram, scale):
    n = gram.shape[1]
    return pl.pallas_call(
        functools.partial(triangle_kernel, scale),
        out_shape=jax.ShapeDtypeStruct((n, n), F32),
        in_specs=[VMEM],
        out_specs=VMEM,
        compiler_params=SMALL,
        name="triangle",
    )(gram)


def local(state_field, start_basis):
    x_cells, y_cells, species, z_cells = state_field.shape
    rank_kept = start_basis.shape[1]
    unfolded = state_field.reshape(x_cells * y_cells * species, z_cells)
    x_parts = lax.axis_size("gx")
    place = lax.axis_index("gx").astype(jnp.int32).reshape(1)
    mine, other, held = local_gram(place, pltpu.with_memory_space_constraint(unfolded, pltpu.HBM))
    mine = summed(mine + partner(other, "gx", 1), skip_core=True)
    other = partner(mine, "gx", 1)
    basis, image, gram = begin(place, mine, other, start_basis.T)
    ahead = contract_ahead(place, held, image, x_cells, y_cells, species, x_parts)
    far = [partner(piece, "gx", d + x_parts // 2) for d, piece in enumerate(ahead)]
    basis, ahead = lax.optimization_barrier((basis, ahead))
    basis_rows, factor = finish(basis, gram)
    core_tensor, *near = contract(place, held, basis_rows, x_cells, y_cells, species, x_parts)
    near = [partner(piece, "gx", d) if d else piece for d, piece in enumerate(near)]
    gram_x = summed(product(place, factor, near + far))
    column_count = y_cells * lax.axis_size("gy") * species * rank_kept
    x_triangle = triangle(gram_x, 1.0 / column_count**0.5)
    return (core_tensor.reshape(x_cells, y_cells, species * rank_kept), basis_rows.T, x_triangle)


def solution(mesh):
    return jax.shard_map(
        local,
        mesh=mesh,
        in_specs=(P("gx", "gy", None, None), P()),
        out_specs=(P("gx", "gy", None), P(), P()),
        check_vma=False,
    )
```

time: 98.9 us -> 84.4 us (0.85)
  waiting for transfers between devices: 41 us -> 36.6 us
  Pallas kernels: 31.1 us -> 26.9 us
  other arithmetic: 4.16 us -> 0.08 us
  local copies, waits for them, and re-layouts: 2.78 us -> 0.76 us
    ppermute x14, waiting for transfers between devices: 41 us -> 36.6 us  [partner(): lax.ppermute(value, axis, [(i, i ^ mask) for i in range(lax.axis_size(axi...]
    pallas_call x1, Pallas kernels: 8.87 us -> 4.42 us  [contract(): pl.pallas_call(functools.partial(core_kernel, species, y_cells), grid=(st...]
    dynamic_slice x1 -> x0, local copies, waits for them, and re-layouts: 2 us -> none  [local(): piece = lax.dynamic_slice_in_dim(by_y, (place ^ d) * share, share, axis=0)]
    select_n x2 -> x0, other arithmetic: 1.64 us -> none  [the longest x1 0.95 us: local(): jnp.where(even, halves[1], halves[0])]
    add x9, other arithmetic: 1.56 us -> 0.07 us  [summed(): value = value + partner(value, axis, bit)]
    pallas_call x3 -> x5, Pallas kernels: 16.7 us -> 17.7 us  [the longest x1 4.99 us: local_gram(): pl.pallas_call(functools.partial(gram_kernel, cuts), out_shape=[out, out,...]
where the time goes in v3:
time: 84.4 us; the launch traced here: 84.3 us
  waiting for transfers between devices  36.6 us (43%)
  Pallas kernels  26.9 us (32%)
  starting transfers between devices  19.3 us (23%)
    ppermute x14, waiting for transfers between devices, partner(): lax.ppermute(value, axis, [(i, i ^ mask) for i in range(lax.axis_size(axi...  36.6 us
    ppermute x14, starting transfers between devices, partner(): lax.ppermute(value, axis, [(i, i ^ mask) for i in range(lax.axis_size(axi...  19.3 us
    pallas_call x1, Pallas kernels, local_gram(): pl.pallas_call(functools.partial(gram_kernel, cuts), out_shape=[out, out,...  4.99 us
    pallas_call x1, Pallas kernels, triangle(): pl.pallas_call(functools.partial(triangle_kernel, scale), out_shape=jax.S...  4.8 us
    pallas_call x1, Pallas kernels, contract(): pl.pallas_call(functools.partial(core_kernel, species, y_cells), grid=(st...  4.42 us
    pallas_call x1, Pallas kernels, finish(): pl.pallas_call(finish_kernel, out_shape=[jax.ShapeDtypeStruct((rank, z),...  3.91 us
    pallas_call x1, Pallas kernels, begin(): pl.pallas_call(begin_kernel, out_shape=[rows, rows, jax.ShapeDtypeStruct(...  3.9 us
    pallas_call x1, Pallas kernels, contract_ahead(): pl.pallas_call(functools.partial(ahead_kernel, chunks, species), out_shap...  3.48 us
  transfers between devices with their start and end apart: 14, of which 13 were waited for; matrix products, arithmetic and copies ran while one was open for 0% of the time, Pallas kernels for 0%

profile of v3, /device:TPU:0, one launch (start us, length us, event | category | flops | bytes accessed | tf_op | source)
XLA Modules:
  0.0 84.3 jit_solution(5412904357754498845)
XLA Ops:
  0.6 0.0 copy-start.1
  0.6 5.0 %gram.1 = (f32[136,128]{1,0:T(8,128)S(1)}, f32[136,128]{1,0:T(8,128)S(1)}, f32[8192,256]{1,0:T(8,128)S(1)}) custom-call(s32[1]{0:T(128)} %bitcast.place, f32[8192,256]{1,0:T(8,128)} %bitcast.9), custom_call_target="tpu_custom_call" | custom-call | tf_op jit(solution)/shard_map/gram/pallas_call | solution.py:197
  5.6 0.6 collective-permute-start
  6.2 0.9 %collective-permute-done = f32[136,128]{1,0:T(8,128)S(1)} collective-permute-done((f32[136,128]{1,0:T(8,128)S(1)}, f32[136,128]{1,0:T(8,128)S(1)}, u32[]{:S(2)}, u32[]{:S(2)}) %collective-permute-start) | collective-permute-done | bytes 69664 | tf_op jit(solution)/shard_map/ppermute | solution.py:28
  7.1 2.9 %collective-permute-start.1 = (f32[136,128]{1,0:T(8,128)S(1)}, f32[136,128]{1,0:T(8,128)S(1)}, u32[]{:S(2)}, u32[]{:S(2)}) collective-permute-start(f32[136,128]{1,0:T(8,128)S(1)} %add.30), channel_id=1, source_target_pairs={{0,16},{8,24},{16,0},{24,8},{1,17},{9,25},{17,1},{25,9},{2,18},{10... | collective-permute-start | bytes 208904 | tf_op jit(solution)/shard_map/ppermute | solution.py:28
  10.0 2.5 %collective-permute-done.1 = f32[136,128]{1,0:T(8,128)S(1)} collective-permute-done((f32[136,128]{1,0:T(8,128)S(1)}, f32[136,128]{1,0:T(8,128)S(1)}, u32[]{:S(2)}, u32[]{:S(2)}) %collective-permute-start.1) | collective-permute-done | bytes 69664 | tf_op jit(solution)/shard_map/ppermute | solution.py:28
  12.5 1.9 %collective-permute-start.2 = (f32[136,128]{1,0:T(8,128)S(1)}, f32[136,128]{1,0:T(8,128)S(1)}, u32[]{:S(2)}, u32[]{:S(2)}) collective-permute-start(f32[136,128]{1,0:T(8,128)S(1)} %add.31), channel_id=1, source_target_pairs={{0,1},{1,0},{2,3},{3,2},{4,5},{5,4},{6,7},{7,6},{8,9},{9,8},{10,11... | collective-permute-start | bytes 208904 | tf_op jit(solution)/shard_map/ppermute | solution.py:28
  14.4 2.5 %collective-permute-done.2 = f32[136,128]{1,0:T(8,128)S(1)} collective-permute-done((f32[136,128]{1,0:T(8,128)S(1)}, f32[136,128]{1,0:T(8,128)S(1)}, u32[]{:S(2)}, u32[]{:S(2)}) %collective-permute-start.2) | collective-permute-done | bytes 69664 | tf_op jit(solution)/shard_map/ppermute | solution.py:28
  16.9 2.0 %collective-permute-start.3 = (f32[136,128]{1,0:T(8,128)S(1)}, f32[136,128]{1,0:T(8,128)S(1)}, u32[]{:S(2)}, u32[]{:S(2)}) collective-permute-start(f32[136,128]{1,0:T(8,128)S(1)} %add.32), channel_id=1, source_target_pairs={{0,2},{1,3},{2,0},{3,1},{4,6},{5,7},{6,4},{7,5},{8,10},{9,11},{10,... | collective-permute-start | bytes 208904 | tf_op jit(solution)/shard_map/ppermute | solution.py:28
  18.9 2.4 %collective-permute-done.3 = f32[136,128]{1,0:T(8,128)S(1)} collective-permute-done((f32[136,128]{1,0:T(8,128)S(1)}, f32[136,128]{1,0:T(8,128)S(1)}, u32[]{:S(2)}, u32[]{:S(2)}) %collective-permute-start.3) | collective-permute-done | bytes 69664 | tf_op jit(solution)/shard_map/ppermute | solution.py:28
  21.3 3.7 %collective-permute-start.4 = (f32[136,128]{1,0:T(8,128)S(1)}, f32[136,128]{1,0:T(8,128)S(1)}, u32[]{:S(2)}, u32[]{:S(2)}) collective-permute-start(f32[136,128]{1,0:T(8,128)S(1)} %add.33), channel_id=1, source_target_pairs={{0,4},{1,5},{2,6},{3,7},{4,0},{5,1},{6,2},{7,3},{8,12},{9,13},{10,... | collective-permute-start | bytes 208904 | tf_op jit(solution)/shard_map/ppermute | solution.py:28
  25.0 3.0 %collective-permute-done.4 = f32[136,128]{1,0:T(8,128)S(1)} collective-permute-done((f32[136,128]{1,0:T(8,128)S(1)}, f32[136,128]{1,0:T(8,128)S(1)}, u32[]{:S(2)}, u32[]{:S(2)}) %collective-permute-start.4) | collective-permute-done | bytes 69664 | tf_op jit(solution)/shard_map/ppermute | solution.py:28
  28.1 0.1 collective-permute-start.5
  28.1 1.2 %collective-permute-done.5.other = f32[136,128]{1,0:T(8,128)S(1)} collective-permute-done((f32[136,128]{1,0:T(8,128)S(1)}, f32[136,128]{1,0:T(8,128)S(1)}, u32[]{:S(2)}, u32[]{:S(2)}) %collective-permute-start.5) | collective-permute-done | bytes 69664 | tf_op jit(solution)/shard_map/ppermute | solution.py:28
  29.4 0.0 copy-done.1
  29.4 3.9 %begin.1 = (f32[32,256]{1,0:T(8,128)S(1)}, f32[32,256]{1,0:T(8,128)S(1)}, f32[256,256]{1,0:T(8,128)S(1)}) custom-call(s32[1]{0:T(128)} %bitcast.place, f32[136,128]{1,0:T(8,128)S(1)} %add.34.mine, f32[136,128]{1,0:T(8,128)S(1)} %collective-permute-done.5.other, f32[32,256]{1,0:T(8,128)S(1)} %bitcast.8), custom_call_target="tpu_custom_call" | custom-call | tf_op jit(solution)/shard_map/begin/pallas_call | solution.py:235
  33.3 3.5 %ahead.1 = (f32[4,32,512]{2,1,0:T(8,128)S(1)}, f32[4,32,512]{2,1,0:T(8,128)S(1)}) custom-call(s32[1]{0:T(128)} %bitcast.place, f32[32,256,256]{2,1,0:T(8,128)S(1)} %bitcast.6, f32[32,256]{1,0:T(8,128)S(1)} %get-tuple-element.21.image), custom_call_target="tpu_custom_call" | custom-call | tf_op jit(solution)/shard_map/ahead/pallas_call | solution.py:298
  36.8 3.9 %finish.1 = (f32[32,256]{1,0:T(8,128)}, f32[32,32]{1,0:T(8,128)S(1)}) custom-call(f32[32,256]{1,0:T(8,128)S(1)} %get-tuple-element.24.basis, f32[256,256]{1,0:T(8,128)S(1)} %get-tuple-element.25.gram), custom_call_target="tpu_custom_call" | custom-call | flops 1073741824 | bytes 16777216 | tf_op jit(solution)/shard_map/finish/pallas_call | solution.py:258
  40.7 0.0 copy-start
  40.7 0.8 copy-done
  41.4 4.4 %core.1 = (f32[512,512]{1,0:T(8,128)}, f32[4,32,512]{2,1,0:T(8,128)S(1)}, f32[4,32,512]{2,1,0:T(8,128)S(1)}) custom-call(s32[1]{0:T(128)} %bitcast.place, f32[8192,256]{1,0:T(8,128)S(1)} %get-tuple-element.17.field, f32[32,256]{1,0:T(8,128)S(1)} %copy-done), custom_call_target="tpu_custom_call" | custom-call | flops 2147483648 | bytes 16777216 | tf_op jit(solution)/shard_map/core/pallas_call | solution.py:341
  45.9 0.2 collective-permute-start.6
  46.0 1.6 %collective-permute-start.7 = (f32[4,32,512]{2,1,0:T(8,128)S(1)}, f32[4,32,512]{2,1,0:T(8,128)S(1)}, u32[]{:S(2)}, u32[]{:S(2)}) collective-permute-start(f32[4,32,512]{2,1,0:T(8,128)S(1)} %get-tuple-element.22), channel_id=1, source_target_pairs={{0,16},{8,24},{16,0},{24,8},{1,17},{9,25},{17,1},{25,9},{2,18},{10... | collective-permute-start | bytes 786440 | tf_op jit(solution)/shard_map/ppermute | solution.py:28
  47.6 0.1 collective-permute-start.8
  47.7 0.0 collective-permute-done.6.refs_1_
  47.7 7.5 %collective-permute-done.7.refs_2_ = f32[4,32,512]{2,1,0:T(8,128)S(1)} collective-permute-done((f32[4,32,512]{2,1,0:T(8,128)S(1)}, f32[4,32,512]{2,1,0:T(8,128)S(1)}, u32[]{:S(2)}, u32[]{:S(2)}) %collective-permute-start.7) | collective-permute-done | bytes 262176 | tf_op jit(solution)/shard_map/ppermute | solution.py:28
  55.2 4.4 %collective-permute-done.8.refs_3_ = f32[4,32,512]{2,1,0:T(8,128)S(1)} collective-permute-done((f32[4,32,512]{2,1,0:T(8,128)S(1)}, f32[4,32,512]{2,1,0:T(8,128)S(1)}, u32[]{:S(2)}, u32[]{:S(2)}) %collective-permute-start.8) | collective-permute-done | bytes 262176 | tf_op jit(solution)/shard_map/ppermute | solution.py:28
  59.6 1.4 %product.1 = f32[72,128]{1,0:T(8,128)S(1)} custom-call(s32[1]{0:T(128)} %bitcast.place, f32[32,32]{1,0:T(8,128)S(1)} %get-tuple-element.28.factor, f32[4,32,512]{2,1,0:T(8,128)S(1)} %get-tuple-element.29.refs_0_, f32[4,32,512]{2,1,0:T(8,128)S(1)} %collective-permute-done.6.refs_1_, f32[4,32,512]{2,1,0:T(8,128)S(1)} %collective-permute-done.7.refs_2_, ...), custom_call_target="tpu_custom_call" | custom-call | tf_op jit(solution)/shard_map/product/pallas_call | solution.py:411
  61.0 0.5 collective-permute-start.9
  61.4 0.9 %collective-permute-done.9 = f32[72,128]{1,0:T(8,128)S(1)} collective-permute-done((f32[72,128]{1,0:T(8,128)S(1)}, f32[72,128]{1,0:T(8,128)S(1)}, u32[]{:S(2)}, u32[]{:S(2)}) %collective-permute-start.9) | collective-permute-done | bytes 36896 | tf_op jit(solution)/shard_map/ppermute | solution.py:28
  62.3 1.6 %collective-permute-start.10 = (f32[72,128]{1,0:T(8,128)S(1)}, f32[72,128]{1,0:T(8,128)S(1)}, u32[]{:S(2)}, u32[]{:S(2)}) collective-permute-start(f32[72,128]{1,0:T(8,128)S(1)} %add.35), channel_id=1, source_target_pairs={{0,16},{8,24},{16,0},{24,8},{1,17},{9,25},{17,1},{25,9},{2,18},{10... | collective-permute-start | bytes 110600 | tf_op jit(solution)/shard_map/ppermute | solution.py:28
  63.9 2.4 %collective-permute-done.10 = f32[72,128]{1,0:T(8,128)S(1)} collective-permute-done((f32[72,128]{1,0:T(8,128)S(1)}, f32[72,128]{1,0:T(8,128)S(1)}, u32[]{:S(2)}, u32[]{:S(2)}) %collective-permute-start.10) | collective-permute-done | bytes 36896 | tf_op jit(solution)/shard_map/ppermute | solution.py:28
  66.3 1.5 %collective-permute-start.11 = (f32[72,128]{1,0:T(8,128)S(1)}, f32[72,128]{1,0:T(8,128)S(1)}, u32[]{:S(2)}, u32[]{:S(2)}) collective-permute-start(f32[72,128]{1,0:T(8,128)S(1)} %add.36), channel_id=1, source_target_pairs={{0,1},{1,0},{2,3},{3,2},{4,5},{5,4},{6,7},{7,6},{8,9},{9,8},{10,11... | collective-permute-start | bytes 110600 | tf_op jit(solution)/shard_map/ppermute | solution.py:28
  67.7 2.5 %collective-permute-done.11 = f32[72,128]{1,0:T(8,128)S(1)} collective-permute-done((f32[72,128]{1,0:T(8,128)S(1)}, f32[72,128]{1,0:T(8,128)S(1)}, u32[]{:S(2)}, u32[]{:S(2)}) %collective-permute-start.11) | collective-permute-done | bytes 36896 | tf_op jit(solution)/shard_map/ppermute | solution.py:28
  70.2 0.5 collective-permute-start.12
  70.8 3.4 %collective-permute-done.12 = f32[72,128]{1,0:T(8,128)S(1)} collective-permute-done((f32[72,128]{1,0:T(8,128)S(1)}, f32[72,128]{1,0:T(8,128)S(1)}, u32[]{:S(2)}, u32[]{:S(2)}) %collective-permute-start.12) | collective-permute-done | bytes 36896 | tf_op jit(solution)/shard_map/ppermute | solution.py:28
  74.2 2.3 %collective-permute-start.13 = (f32[72,128]{1,0:T(8,128)S(1)}, f32[72,128]{1,0:T(8,128)S(1)}, u32[]{:S(2)}, u32[]{:S(2)}) collective-permute-start(f32[72,128]{1,0:T(8,128)S(1)} %add.38), channel_id=1, source_target_pairs={{0,4},{1,5},{2,6},{3,7},{4,0},{5,1},{6,2},{7,3},{8,12},{9,13},{10,... | collective-permute-start | bytes 110600 | tf_op jit(solution)/shard_map/ppermute | solution.py:28
  76.5 2.9 %collective-permute-done.13 = f32[72,128]{1,0:T(8,128)S(1)} collective-permute-done((f32[72,128]{1,0:T(8,128)S(1)}, f32[72,128]{1,0:T(8,128)S(1)}, u32[]{:S(2)}, u32[]{:S(2)}) %collective-permute-start.13) | collective-permute-done | bytes 36896 | tf_op jit(solution)/shard_map/ppermute | solution.py:28
  79.4 4.8 %triangle.1 = f32[128,128]{1,0:T(8,128)} custom-call(f32[72,128]{1,0:T(8,128)S(1)} %add.39.gram), custom_call_target="tpu_custom_call" | custom-call | tf_op jit(solution)/shard_map/triangle/pallas_call | solution.py:432
  (10 shorter events, 0.1 us)
Async XLA Ops:
  0.6 28.8 %copy-start.1 = (f32[256,32]{0,1:T(8,128)S(1)}, f32[256,32]{0,1:T(8,128)}, u32[]{:S(2)}) copy-start(f32[256,32]{0,1:T(8,128)} %param.3) | copy-start | bytes 98308
  5.6 1.5 %collective-permute-start = (f32[136,128]{1,0:T(8,128)S(1)}, f32[136,128]{1,0:T(8,128)S(1)}, u32[]{:S(2)}, u32[]{:S(2)}) collective-permute-start(f32[136,128]{1,0:T(8,128)S(1)} %get-tuple-element.19), channel_id=1, source_target_pairs={{0,8},{8,0},{16,24},{24,16},{1,9},{9,1},{17,25},{25,17},{2,10},{10... | collective-permute-start | bytes 208904 | tf_op jit(solution)/shard_map/ppermute | solution.py:28
  7.1 5.4 %collective-permute-start.1 = (f32[136,128]{1,0:T(8,128)S(1)}, f32[136,128]{1,0:T(8,128)S(1)}, u32[]{:S(2)}, u32[]{:S(2)}) collective-permute-start(f32[136,128]{1,0:T(8,128)S(1)} %add.30), channel_id=1, source_target_pairs={{0,16},{8,24},{16,0},{24,8},{1,17},{9,25},{17,1},{25,9},{2,18},{10... | collective-permute-start | bytes 208904 | tf_op jit(solution)/shard_map/ppermute | solution.py:28
  12.5 4.4 %collective-permute-start.2 = (f32[136,128]{1,0:T(8,128)S(1)}, f32[136,128]{1,0:T(8,128)S(1)}, u32[]{:S(2)}, u32[]{:S(2)}) collective-permute-start(f32[136,128]{1,0:T(8,128)S(1)} %add.31), channel_id=1, source_target_pairs={{0,1},{1,0},{2,3},{3,2},{4,5},{5,4},{6,7},{7,6},{8,9},{9,8},{10,11... | collective-permute-start | bytes 208904 | tf_op jit(solution)/shard_map/ppermute | solution.py:28
  16.9 4.4 %collective-permute-start.3 = (f32[136,128]{1,0:T(8,128)S(1)}, f32[136,128]{1,0:T(8,128)S(1)}, u32[]{:S(2)}, u32[]{:S(2)}) collective-permute-start(f32[136,128]{1,0:T(8,128)S(1)} %add.32), channel_id=1, source_target_pairs={{0,2},{1,3},{2,0},{3,1},{4,6},{5,7},{6,4},{7,5},{8,10},{9,11},{10,... | collective-permute-start | bytes 208904 | tf_op jit(solution)/shard_map/ppermute | solution.py:28
  21.3 6.7 %collective-permute-start.4 = (f32[136,128]{1,0:T(8,128)S(1)}, f32[136,128]{1,0:T(8,128)S(1)}, u32[]{:S(2)}, u32[]{:S(2)}) collective-permute-start(f32[136,128]{1,0:T(8,128)S(1)} %add.33), channel_id=1, source_target_pairs={{0,4},{1,5},{2,6},{3,7},{4,0},{5,1},{6,2},{7,3},{8,12},{9,13},{10,... | collective-permute-start | bytes 208904 | tf_op jit(solution)/shard_map/ppermute | solution.py:28
  28.1 1.3 %collective-permute-start.5 = (f32[136,128]{1,0:T(8,128)S(1)}, f32[136,128]{1,0:T(8,128)S(1)}, u32[]{:S(2)}, u32[]{:S(2)}) collective-permute-start(f32[136,128]{1,0:T(8,128)S(1)} %add.34.mine), channel_id=1, source_target_pairs={{0,8},{8,0},{16,24},{24,16},{1,9},{9,1},{17,25},{25,17},{2,10},{10... | collective-permute-start | bytes 208904 | tf_op jit(solution)/shard_map/ppermute | solution.py:28
  40.7 0.8 copy-start
  45.9 1.9 %collective-permute-start.6 = (f32[4,32,512]{2,1,0:T(8,128)S(1)}, f32[4,32,512]{2,1,0:T(8,128)S(1)}, u32[]{:S(2)}, u32[]{:S(2)}) collective-permute-start(f32[4,32,512]{2,1,0:T(8,128)S(1)} %get-tuple-element.30), channel_id=1, source_target_pairs={{0,8},{8,0},{16,24},{24,16},{1,9},{9,1},{17,25},{25,17},{2,10},{10... | collective-permute-start | bytes 786440 | tf_op jit(solution)/shard_map/ppermute | solution.py:28
  46.0 9.2 %collective-permute-start.7 = (f32[4,32,512]{2,1,0:T(8,128)S(1)}, f32[4,32,512]{2,1,0:T(8,128)S(1)}, u32[]{:S(2)}, u32[]{:S(2)}) collective-permute-start(f32[4,32,512]{2,1,0:T(8,128)S(1)} %get-tuple-element.22), channel_id=1, source_target_pairs={{0,16},{8,24},{16,0},{24,8},{1,17},{9,25},{17,1},{25,9},{2,18},{10... | collective-permute-start | bytes 786440 | tf_op jit(solution)/shard_map/ppermute | solution.py:28
  47.6 12.0 %collective-permute-start.8 = (f32[4,32,512]{2,1,0:T(8,128)S(1)}, f32[4,32,512]{2,1,0:T(8,128)S(1)}, u32[]{:S(2)}, u32[]{:S(2)}) collective-permute-start(f32[4,32,512]{2,1,0:T(8,128)S(1)} %get-tuple-element.23), channel_id=1, source_target_pairs={{0,24},{8,16},{16,8},{24,0},{1,25},{9,17},{17,9},{25,1},{2,26},{10... | collective-permute-start | bytes 786440 | tf_op jit(solution)/shard_map/ppermute | solution.py:28
  61.0 1.3 %collective-permute-start.9 = (f32[72,128]{1,0:T(8,128)S(1)}, f32[72,128]{1,0:T(8,128)S(1)}, u32[]{:S(2)}, u32[]{:S(2)}) collective-permute-start(f32[72,128]{1,0:T(8,128)S(1)} %product.1), channel_id=1, source_target_pairs={{0,8},{8,0},{16,24},{24,16},{1,9},{9,1},{17,25},{25,17},{2,10},{10... | collective-permute-start | bytes 110600 | tf_op jit(solution)/shard_map/ppermute | solution.py:28
  62.3 4.0 %collective-permute-start.10 = (f32[72,128]{1,0:T(8,128)S(1)}, f32[72,128]{1,0:T(8,128)S(1)}, u32[]{:S(2)}, u32[]{:S(2)}) collective-permute-start(f32[72,128]{1,0:T(8,128)S(1)} %add.35), channel_id=1, source_target_pairs={{0,16},{8,24},{16,0},{24,8},{1,17},{9,25},{17,1},{25,9},{2,18},{10... | collective-permute-start | bytes 110600 | tf_op jit(solution)/shard_map/ppermute | solution.py:28
  66.3 4.0 %collective-permute-start.11 = (f32[72,128]{1,0:T(8,128)S(1)}, f32[72,128]{1,0:T(8,128)S(1)}, u32[]{:S(2)}, u32[]{:S(2)}) collective-permute-start(f32[72,128]{1,0:T(8,128)S(1)} %add.36), channel_id=1, source_target_pairs={{0,1},{1,0},{2,3},{3,2},{4,5},{5,4},{6,7},{7,6},{8,9},{9,8},{10,11... | collective-permute-start | bytes 110600 | tf_op jit(solution)/shard_map/ppermute | solution.py:28
  70.2 4.0 %collective-permute-start.12 = (f32[72,128]{1,0:T(8,128)S(1)}, f32[72,128]{1,0:T(8,128)S(1)}, u32[]{:S(2)}, u32[]{:S(2)}) collective-permute-start(f32[72,128]{1,0:T(8,128)S(1)} %add.37), channel_id=1, source_target_pairs={{0,2},{1,3},{2,0},{3,1},{4,6},{5,7},{6,4},{7,5},{8,10},{9,11},{10,... | collective-permute-start | bytes 110600 | tf_op jit(solution)/shard_map/ppermute | solution.py:28
  74.2 5.3 %collective-permute-start.13 = (f32[72,128]{1,0:T(8,128)S(1)}, f32[72,128]{1,0:T(8,128)S(1)}, u32[]{:S(2)}, u32[]{:S(2)}) collective-permute-start(f32[72,128]{1,0:T(8,128)S(1)} %add.38), channel_id=1, source_target_pairs={{0,4},{1,5},{2,6},{3,7},{4,0},{5,1},{6,2},{7,3},{8,12},{9,13},{10,... | collective-permute-start | bytes 110600 | tf_op jit(solution)/shard_map/ppermute | solution.py:28

commit v4 on v3

--- a/solution.py
+++ b/solution.py
@@ -6,6 +6,7 @@
 from jax.experimental import pallas as pl
 from jax.experimental.pallas import tpu as pltpu
 from jax.sharding import PartitionSpec as P
+
 
 ITERS = 3
 F32, BF16 = jnp.float32, jnp.bfloat16
@@ -24,14 +25,24 @@
     return [1 << b for b in range(size.bit_length() - 1)]
 
 
-def partner(value, axis, mask):
-    return lax.ppermute(value, axis, [(i, i ^ mask) for i in range(lax.axis_size(axis))])
-
-
-def summed(value, skip_core=False):
-    for axis in ("gx", "gy"):
-        for bit in bits(lax.axis_size(axis))[1 if skip_core and axis == "gx" else 0 :]:
-            value = value + partner(value, axis, bit)
+def partner(value, x_mask, y_mask=0):
+    x_size, y_size = lax.axis_size("gx"), lax.axis_size("gy")
+    pairs = [
+        (x * y_size + y, (x ^ x_mask) * y_size + (y ^ y_mask)) for x in range(x_size) for y in range(y_size)
+    ]
+    return lax.ppermute(value, ("gx", "gy"), pairs)
+
+
+def summed(value):
+    masks = [(bit, 0) for bit in bits(lax.axis_size("gx"))[1:]] + [(0, bit) for bit in bits(lax.axis_size("gy"))]
+    while masks:
+        first, masks = masks[0], masks[1:]
+        near = value + partner(value, *first)
+        if masks:
+            second, masks = masks[0], masks[1:]
+            both = (first[0] ^ second[0], first[1] ^ second[1])
+            near = near + (partner(value, *second) + partner(value, *both))
+        value = near
     return value
 
 
@@ -247,7 +258,7 @@
     r, c = triangle_ids(rank)
     rows, turn = orth_pass(basis[...], jnp.where(r == c, 1.0, 0.0))
     rows = jnp.dot(rows, gram[...], precision=precise, preferred_element_type=F32)
-    for repeat in range(2):
+    for _ in range(2):
         rows, turn = orth_pass(rows, turn)
     out[...] = rows
     factor[...] = turn
@@ -446,16 +457,16 @@
     x_parts = lax.axis_size("gx")
     place = lax.axis_index("gx").astype(jnp.int32).reshape(1)
     mine, other, held = local_gram(place, pltpu.with_memory_space_constraint(unfolded, pltpu.HBM))
-    mine = summed(mine + partner(other, "gx", 1), skip_core=True)
-    other = partner(mine, "gx", 1)
+    mine = summed(mine + partner(other, 1))
+    other = partner(mine, 1)
     basis, image, gram = begin(place, mine, other, start_basis.T)
     ahead = contract_ahead(place, held, image, x_cells, y_cells, species, x_parts)
-    far = [partner(piece, "gx", d + x_parts // 2) for d, piece in enumerate(ahead)]
-    basis, ahead = lax.optimization_barrier((basis, ahead))
+    far = [partner(piece, d + x_parts // 2) for d, piece in enumerate(ahead)]
     basis_rows, factor = finish(basis, gram)
     core_tensor, *near = contract(place, held, basis_rows, x_cells, y_cells, species, x_parts)
-    near = [partner(piece, "gx", d) if d else piece for d, piece in enumerate(near)]
-    gram_x = summed(product(place, factor, near + far))
+    near = [partner(piece, d) if d else piece for d, piece in enumerate(near)]
+    gram_x = product(place, factor, near + far)
+    gram_x = summed(gram_x + partner(gram_x, 1))
     column_count = y_cells * lax.axis_size("gy") * species * rank_kept
     x_triangle = triangle(gram_x, 1.0 / column_count**0.5)
     return (core_tensor.reshape(x_cells, y_cells, species * rank_kept), basis_rows.T, x_triangle)

time: 84.4 us -> 78.4 us (0.929)
  waiting for transfers between devices: 36.6 us -> 29.5 us
  starting transfers between devices: 19.3 us -> 20.4 us
    ppermute x14 -> x18, waiting for transfers between devices: 36.6 us -> 29.5 us  [partner(): return lax.ppermute(value, ('gx', 'gy'), pairs)]
    ppermute x14 -> x18, starting transfers between devices: 19.3 us -> 20.4 us  [partner(): return lax.ppermute(value, ('gx', 'gy'), pairs)]
  transfers between devices with their start and end apart: 14 -> 18, of which waited for: 13 -> 15; matrix products, arithmetic and copies ran while one was open for 0% -> 0% of each run, Pallas kernels for 0% -> 0%
where the time goes in v4:
time: 78.4 us; the launch traced here: 78.3 us
  waiting for transfers between devices  29.5 us (38%)
  Pallas kernels  26.9 us (34%)
  starting transfers between devices  20.4 us (26%)
    ppermute x18, waiting for transfers between devices, partner(): return lax.ppermute(value, ('gx', 'gy'), pairs)  29.5 us
    ppermute x18, starting transfers between devices, partner(): return lax.ppermute(value, ('gx', 'gy'), pairs)  20.4 us
    pallas_call x1, Pallas kernels, local_gram(): pl.pallas_call(functools.partial(gram_kernel, cuts), out_shape=[out, out,...  4.99 us
    pallas_call x1, Pallas kernels, triangle(): pl.pallas_call(functools.partial(triangle_kernel, scale), out_shape=jax.S...  4.8 us
    pallas_call x1, Pallas kernels, contract(): pl.pallas_call(functools.partial(core_kernel, species, y_cells), grid=(st...  4.43 us
    pallas_call x1, Pallas kernels, finish(): pl.pallas_call(finish_kernel, out_shape=[jax.ShapeDtypeStruct((rank, z),...  3.92 us
    pallas_call x1, Pallas kernels, begin(): pl.pallas_call(begin_kernel, out_shape=[rows, rows, jax.ShapeDtypeStruct(...  3.9 us
    pallas_call x1, Pallas kernels, contract_ahead(): pl.pallas_call(functools.partial(ahead_kernel, chunks, species), out_shap...  3.48 us
  transfers between devices with their start and end apart: 18, of which 15 were waited for; matrix products, arithmetic and copies ran while one was open for 0% of the time, Pallas kernels for 0%

profile of v4, /device:TPU:0, one launch (start us, length us, event | category | flops | bytes accessed | tf_op | source)
XLA Modules:
  0.0 78.3 jit_solution(9887325266632295468)
XLA Ops:
  0.6 0.0 copy-start.1
  0.6 5.0 %gram.1 = (f32[136,128]{1,0:T(8,128)S(1)}, f32[136,128]{1,0:T(8,128)S(1)}, f32[8192,256]{1,0:T(8,128)S(1)}) custom-call(s32[1]{0:T(128)} %bitcast.place, f32[8192,256]{1,0:T(8,128)} %bitcast.9), custom_call_target="tpu_custom_call" | custom-call | tf_op jit(solution)/shard_map/gram/pallas_call | solution.py:208
  5.6 0.6 collective-permute-start
  6.2 0.9 %collective-permute-done = f32[136,128]{1,0:T(8,128)S(1)} collective-permute-done((f32[136,128]{1,0:T(8,128)S(1)}, f32[136,128]{1,0:T(8,128)S(1)}, u32[]{:S(2)}, u32[]{:S(2)}) %collective-permute-start) | collective-permute-done | bytes 69664 | tf_op jit(solution)/shard_map/ppermute | solution.py:33
  7.1 3.8 %collective-permute-start.3 = (f32[136,128]{1,0:T(8,128)S(1)}, f32[136,128]{1,0:T(8,128)S(1)}, u32[]{:S(2)}, u32[]{:S(2)}) collective-permute-start(f32[136,128]{1,0:T(8,128)S(1)} %add.42), channel_id=1, source_target_pairs={{0,17},{1,16},{2,19},{3,18},{4,21},{5,20},{6,23},{7,22},{8,25},{9,... | collective-permute-start | bytes 208904 | tf_op jit(solution)/shard_map/ppermute | solution.py:33
  11.0 0.5 collective-permute-start.2
  11.5 0.1 collective-permute-start.1
  11.6 1.9 %collective-permute-done.3 = f32[136,128]{1,0:T(8,128)S(1)} collective-permute-done((f32[136,128]{1,0:T(8,128)S(1)}, f32[136,128]{1,0:T(8,128)S(1)}, u32[]{:S(2)}, u32[]{:S(2)}) %collective-permute-start.3) | collective-permute-done | bytes 69664 | tf_op jit(solution)/shard_map/ppermute | solution.py:33
  13.5 1.8 %collective-permute-done.2 = f32[136,128]{1,0:T(8,128)S(1)} collective-permute-done((f32[136,128]{1,0:T(8,128)S(1)}, f32[136,128]{1,0:T(8,128)S(1)}, u32[]{:S(2)}, u32[]{:S(2)}) %collective-permute-start.2) | collective-permute-done | bytes 69664 | tf_op jit(solution)/shard_map/ppermute | solution.py:33
  15.3 0.5 collective-permute-done.1
  15.8 3.7 %collective-permute-start.6 = (f32[136,128]{1,0:T(8,128)S(1)}, f32[136,128]{1,0:T(8,128)S(1)}, u32[]{:S(2)}, u32[]{:S(2)}) collective-permute-start(f32[136,128]{1,0:T(8,128)S(1)} %add_add_fusion.1), channel_id=1, source_target_pairs={{0,6},{1,7},{2,4},{3,5},{4,2},{5,3},{6,0},{7,1},{8,14},{9,15},{10,... | collective-permute-start | bytes 208904 | tf_op jit(solution)/shard_map/ppermute | solution.py:33
  19.5 0.0 collective-permute-start.5
  19.5 0.8 %collective-permute-start.4 = (f32[136,128]{1,0:T(8,128)S(1)}, f32[136,128]{1,0:T(8,128)S(1)}, u32[]{:S(2)}, u32[]{:S(2)}) collective-permute-start(f32[136,128]{1,0:T(8,128)S(1)} %add_add_fusion.1), channel_id=1, source_target_pairs={{0,2},{1,3},{2,0},{3,1},{4,6},{5,7},{6,4},{7,5},{8,10},{9,11},{10,... | collective-permute-start | bytes 208904 | tf_op jit(solution)/shard_map/ppermute | solution.py:33
  20.3 1.9 %collective-permute-done.6 = f32[136,128]{1,0:T(8,128)S(1)} collective-permute-done((f32[136,128]{1,0:T(8,128)S(1)}, f32[136,128]{1,0:T(8,128)S(1)}, u32[]{:S(2)}, u32[]{:S(2)}) %collective-permute-start.6) | collective-permute-done | bytes 69664 | tf_op jit(solution)/shard_map/ppermute | solution.py:33
  22.1 2.8 %collective-permute-done.5 = f32[136,128]{1,0:T(8,128)S(1)} collective-permute-done((f32[136,128]{1,0:T(8,128)S(1)}, f32[136,128]{1,0:T(8,128)S(1)}, u32[]{:S(2)}, u32[]{:S(2)}) %collective-permute-start.5) | collective-permute-done | bytes 69664 | tf_op jit(solution)/shard_map/ppermute | solution.py:33
  24.9 0.0 collective-permute-done.4
  24.9 0.1 collective-permute-start.7
  25.0 1.2 %collective-permute-done.7.other = f32[136,128]{1,0:T(8,128)S(1)} collective-permute-done((f32[136,128]{1,0:T(8,128)S(1)}, f32[136,128]{1,0:T(8,128)S(1)}, u32[]{:S(2)}, u32[]{:S(2)}) %collective-permute-start.7) | collective-permute-done | bytes 69664 | tf_op jit(solution)/shard_map/ppermute | solution.py:33
  26.3 0.0 copy-done.1
  26.3 3.9 %begin.1 = (f32[32,256]{1,0:T(8,128)S(1)}, f32[32,256]{1,0:T(8,128)S(1)}, f32[256,256]{1,0:T(8,128)S(1)}) custom-call(s32[1]{0:T(128)} %bitcast.place, f32[136,128]{1,0:T(8,128)S(1)} %add_add_fusion.mine, f32[136,128]{1,0:T(8,128)S(1)} %collective-permute-done.7.other, f32[32,256]{1,0:T(8,128)S(1)} %bitcast.8), custom_call_target="tpu_custom_call" | custom-call | tf_op jit(solution)/shard_map/begin/pallas_call | solution.py:246
  30.2 3.9 %finish.1 = (f32[32,256]{1,0:T(8,128)}, f32[32,32]{1,0:T(8,128)S(1)}) custom-call(f32[32,256]{1,0:T(8,128)S(1)} %get-tuple-element.19.basis, f32[256,256]{1,0:T(8,128)S(1)} %get-tuple-element.20.gram), custom_call_target="tpu_custom_call" | custom-call | flops 1073741824 | bytes 16777216 | tf_op jit(solution)/shard_map/finish/pallas_call | solution.py:269
  34.1 0.0 copy-start
  34.1 0.8 copy-done
  34.9 4.4 %core.1 = (f32[512,512]{1,0:T(8,128)}, f32[4,32,512]{2,1,0:T(8,128)S(1)}, f32[4,32,512]{2,1,0:T(8,128)S(1)}) custom-call(s32[1]{0:T(128)} %bitcast.place, f32[8192,256]{1,0:T(8,128)S(1)} %get-tuple-element.16.field, f32[32,256]{1,0:T(8,128)S(1)} %copy-done), custom_call_target="tpu_custom_call" | custom-call | flops 2147483648 | bytes 16777216 | tf_op jit(solution)/shard_map/core/pallas_call | solution.py:352
  39.3 3.5 %ahead.1 = (f32[4,32,512]{2,1,0:T(8,128)S(1)}, f32[4,32,512]{2,1,0:T(8,128)S(1)}) custom-call(s32[1]{0:T(128)} %bitcast.place, f32[32,256,256]{2,1,0:T(8,128)S(1)} %bitcast.6, f32[32,256]{1,0:T(8,128)S(1)} %get-tuple-element.26.image), custom_call_target="tpu_custom_call" | custom-call | tf_op jit(solution)/shard_map/ahead/pallas_call | solution.py:309
  42.8 1.6 %collective-permute-start.9 = (f32[4,32,512]{2,1,0:T(8,128)S(1)}, f32[4,32,512]{2,1,0:T(8,128)S(1)}, u32[]{:S(2)}, u32[]{:S(2)}) collective-permute-start(f32[4,32,512]{2,1,0:T(8,128)S(1)} %get-tuple-element.27), channel_id=1, source_target_pairs={{0,16},{1,17},{2,18},{3,19},{4,20},{5,21},{6,22},{7,23},{8,24},{9,... | collective-permute-start | bytes 786440 | tf_op jit(solution)/shard_map/ppermute | solution.py:33
  44.3 0.0 collective-permute-start.10
  44.4 0.6 collective-permute-start.8
  45.0 7.0 %collective-permute-done.9.refs_2_ = f32[4,32,512]{2,1,0:T(8,128)S(1)} collective-permute-done((f32[4,32,512]{2,1,0:T(8,128)S(1)}, f32[4,32,512]{2,1,0:T(8,128)S(1)}, u32[]{:S(2)}, u32[]{:S(2)}) %collective-permute-start.9) | collective-permute-done | bytes 262176 | tf_op jit(solution)/shard_map/ppermute | solution.py:33
  52.0 4.0 %collective-permute-done.10.refs_3_ = f32[4,32,512]{2,1,0:T(8,128)S(1)} collective-permute-done((f32[4,32,512]{2,1,0:T(8,128)S(1)}, f32[4,32,512]{2,1,0:T(8,128)S(1)}, u32[]{:S(2)}, u32[]{:S(2)}) %collective-permute-start.10) | collective-permute-done | bytes 262176 | tf_op jit(solution)/shard_map/ppermute | solution.py:33
  56.0 0.0 collective-permute-done.8.refs_1_
  56.0 1.4 %product.1 = f32[72,128]{1,0:T(8,128)S(1)} custom-call(s32[1]{0:T(128)} %bitcast.place, f32[32,32]{1,0:T(8,128)S(1)} %get-tuple-element.23.factor, f32[4,32,512]{2,1,0:T(8,128)S(1)} %get-tuple-element.24.refs_0_, f32[4,32,512]{2,1,0:T(8,128)S(1)} %collective-permute-done.8.refs_1_, f32[4,32,512]{2,1,0:T(8,128)S(1)} %collective-permute-done.9.refs_2_, ...), custom_call_target="tpu_custom_call" | custom-call | tf_op jit(solution)/shard_map/product/pallas_call | solution.py:422
  57.4 0.6 collective-permute-start.11
  58.1 0.9 %collective-permute-done.11 = f32[72,128]{1,0:T(8,128)S(1)} collective-permute-done((f32[72,128]{1,0:T(8,128)S(1)}, f32[72,128]{1,0:T(8,128)S(1)}, u32[]{:S(2)}, u32[]{:S(2)}) %collective-permute-start.11) | collective-permute-done | bytes 36896 | tf_op jit(solution)/shard_map/ppermute | solution.py:33
  58.9 1.5 %collective-permute-start.14 = (f32[72,128]{1,0:T(8,128)S(1)}, f32[72,128]{1,0:T(8,128)S(1)}, u32[]{:S(2)}, u32[]{:S(2)}) collective-permute-start(f32[72,128]{1,0:T(8,128)S(1)} %add.49), channel_id=1, source_target_pairs={{0,17},{1,16},{2,19},{3,18},{4,21},{5,20},{6,23},{7,22},{8,25},{9,... | collective-permute-start | bytes 110600 | tf_op jit(solution)/shard_map/ppermute | solution.py:33
  60.5 1.4 %collective-permute-start.13 = (f32[72,128]{1,0:T(8,128)S(1)}, f32[72,128]{1,0:T(8,128)S(1)}, u32[]{:S(2)}, u32[]{:S(2)}) collective-permute-start(f32[72,128]{1,0:T(8,128)S(1)} %add.49), channel_id=1, source_target_pairs={{0,1},{1,0},{2,3},{3,2},{4,5},{5,4},{6,7},{7,6},{8,9},{9,8},{10,11... | collective-permute-start | bytes 110600 | tf_op jit(solution)/shard_map/ppermute | solution.py:33
  61.9 0.5 collective-permute-start.12
  62.4 1.4 %collective-permute-done.14 = f32[72,128]{1,0:T(8,128)S(1)} collective-permute-done((f32[72,128]{1,0:T(8,128)S(1)}, f32[72,128]{1,0:T(8,128)S(1)}, u32[]{:S(2)}, u32[]{:S(2)}) %collective-permute-start.14) | collective-permute-done | bytes 36896 | tf_op jit(solution)/shard_map/ppermute | solution.py:33
  63.8 0.6 collective-permute-done.13
  64.4 1.4 %collective-permute-done.12 = f32[72,128]{1,0:T(8,128)S(1)} collective-permute-done((f32[72,128]{1,0:T(8,128)S(1)}, f32[72,128]{1,0:T(8,128)S(1)}, u32[]{:S(2)}, u32[]{:S(2)}) %collective-permute-start.12) | collective-permute-done | bytes 36896 | tf_op jit(solution)/shard_map/ppermute | solution.py:33
  65.9 2.7 %collective-permute-start.17 = (f32[72,128]{1,0:T(8,128)S(1)}, f32[72,128]{1,0:T(8,128)S(1)}, u32[]{:S(2)}, u32[]{:S(2)}) collective-permute-start(f32[72,128]{1,0:T(8,128)S(1)} %add_add_fusion.3), channel_id=1, source_target_pairs={{0,6},{1,7},{2,4},{3,5},{4,2},{5,3},{6,0},{7,1},{8,14},{9,15},{10,... | collective-permute-start | bytes 110600 | tf_op jit(solution)/shard_map/ppermute | solution.py:33
  68.6 0.0 collective-permute-start.16
  68.6 1.7 %collective-permute-start.15 = (f32[72,128]{1,0:T(8,128)S(1)}, f32[72,128]{1,0:T(8,128)S(1)}, u32[]{:S(2)}, u32[]{:S(2)}) collective-permute-start(f32[72,128]{1,0:T(8,128)S(1)} %add_add_fusion.3), channel_id=1, source_target_pairs={{0,2},{1,3},{2,0},{3,1},{4,6},{5,7},{6,4},{7,5},{8,10},{9,11},{10,... | collective-permute-start | bytes 110600 | tf_op jit(solution)/shard_map/ppermute | solution.py:33
  70.3 1.4 %collective-permute-done.17 = f32[72,128]{1,0:T(8,128)S(1)} collective-permute-done((f32[72,128]{1,0:T(8,128)S(1)}, f32[72,128]{1,0:T(8,128)S(1)}, u32[]{:S(2)}, u32[]{:S(2)}) %collective-permute-start.17) | collective-permute-done | bytes 36896 | tf_op jit(solution)/shard_map/ppermute | solution.py:33
  71.8 1.7 %collective-permute-done.16 = f32[72,128]{1,0:T(8,128)S(1)} collective-permute-done((f32[72,128]{1,0:T(8,128)S(1)}, f32[72,128]{1,0:T(8,128)S(1)}, u32[]{:S(2)}, u32[]{:S(2)}) %collective-permute-start.16) | collective-permute-done | bytes 36896 | tf_op jit(solution)/shard_map/ppermute | solution.py:33
  73.4 0.0 collective-permute-done.15
  73.5 4.8 %triangle.1 = f32[128,128]{1,0:T(8,128)} custom-call(f32[72,128]{1,0:T(8,128)S(1)} %add_add_fusion.2.gram), custom_call_target="tpu_custom_call" | custom-call | tf_op jit(solution)/shard_map/triangle/pallas_call | solution.py:443
  (6 shorter events, 0.1 us)
Async XLA Ops:
  0.6 25.6 %copy-start.1 = (f32[256,32]{0,1:T(8,128)S(1)}, f32[256,32]{0,1:T(8,128)}, u32[]{:S(2)}) copy-start(f32[256,32]{0,1:T(8,128)} %param.3) | copy-start | bytes 98308
  5.6 1.5 %collective-permute-start = (f32[136,128]{1,0:T(8,128)S(1)}, f32[136,128]{1,0:T(8,128)S(1)}, u32[]{:S(2)}, u32[]{:S(2)}) collective-permute-start(f32[136,128]{1,0:T(8,128)S(1)} %get-tuple-element.18), channel_id=1, source_target_pairs={{0,8},{1,9},{2,10},{3,11},{4,12},{5,13},{6,14},{7,15},{8,0},{9,1},... | collective-permute-start | bytes 208904 | tf_op jit(solution)/shard_map/ppermute | solution.py:33
  7.1 6.3 %collective-permute-start.3 = (f32[136,128]{1,0:T(8,128)S(1)}, f32[136,128]{1,0:T(8,128)S(1)}, u32[]{:S(2)}, u32[]{:S(2)}) collective-permute-start(f32[136,128]{1,0:T(8,128)S(1)} %add.42), channel_id=1, source_target_pairs={{0,17},{1,16},{2,19},{3,18},{4,21},{5,20},{6,23},{7,22},{8,25},{9,... | collective-permute-start | bytes 208904 | tf_op jit(solution)/shard_map/ppermute | solution.py:33
  11.0 4.3 %collective-permute-start.2 = (f32[136,128]{1,0:T(8,128)S(1)}, f32[136,128]{1,0:T(8,128)S(1)}, u32[]{:S(2)}, u32[]{:S(2)}) collective-permute-start(f32[136,128]{1,0:T(8,128)S(1)} %add.42), channel_id=1, source_target_pairs={{0,1},{1,0},{2,3},{3,2},{4,5},{5,4},{6,7},{7,6},{8,9},{9,8},{10,11... | collective-permute-start | bytes 208904 | tf_op jit(solution)/shard_map/ppermute | solution.py:33
  11.5 4.3 %collective-permute-start.1 = (f32[136,128]{1,0:T(8,128)S(1)}, f32[136,128]{1,0:T(8,128)S(1)}, u32[]{:S(2)}, u32[]{:S(2)}) collective-permute-start(f32[136,128]{1,0:T(8,128)S(1)} %add.42), channel_id=1, source_target_pairs={{0,16},{1,17},{2,18},{3,19},{4,20},{5,21},{6,22},{7,23},{8,24},{9,... | collective-permute-start | bytes 208904 | tf_op jit(solution)/shard_map/ppermute | solution.py:33
  15.8 6.3 %collective-permute-start.6 = (f32[136,128]{1,0:T(8,128)S(1)}, f32[136,128]{1,0:T(8,128)S(1)}, u32[]{:S(2)}, u32[]{:S(2)}) collective-permute-start(f32[136,128]{1,0:T(8,128)S(1)} %add_add_fusion.1), channel_id=1, source_target_pairs={{0,6},{1,7},{2,4},{3,5},{4,2},{5,3},{6,0},{7,1},{8,14},{9,15},{10,... | collective-permute-start | bytes 208904 | tf_op jit(solution)/shard_map/ppermute | solution.py:33
  19.5 5.5 %collective-permute-start.5 = (f32[136,128]{1,0:T(8,128)S(1)}, f32[136,128]{1,0:T(8,128)S(1)}, u32[]{:S(2)}, u32[]{:S(2)}) collective-permute-start(f32[136,128]{1,0:T(8,128)S(1)} %add_add_fusion.1), channel_id=1, source_target_pairs={{0,4},{1,5},{2,6},{3,7},{4,0},{5,1},{6,2},{7,3},{8,12},{9,13},{10,... | collective-permute-start | bytes 208904 | tf_op jit(solution)/shard_map/ppermute | solution.py:33
  19.5 5.5 %collective-permute-start.4 = (f32[136,128]{1,0:T(8,128)S(1)}, f32[136,128]{1,0:T(8,128)S(1)}, u32[]{:S(2)}, u32[]{:S(2)}) collective-permute-start(f32[136,128]{1,0:T(8,128)S(1)} %add_add_fusion.1), channel_id=1, source_target_pairs={{0,2},{1,3},{2,0},{3,1},{4,6},{5,7},{6,4},{7,5},{8,10},{9,11},{10,... | collective-permute-start | bytes 208904 | tf_op jit(solution)/shard_map/ppermute | solution.py:33
  24.9 1.3 %collective-permute-start.7 = (f32[136,128]{1,0:T(8,128)S(1)}, f32[136,128]{1,0:T(8,128)S(1)}, u32[]{:S(2)}, u32[]{:S(2)}) collective-permute-start(f32[136,128]{1,0:T(8,128)S(1)} %add_add_fusion.mine), channel_id=1, source_target_pairs={{0,8},{1,9},{2,10},{3,11},{4,12},{5,13},{6,14},{7,15},{8,0},{9,1},... | collective-permute-start | bytes 208904 | tf_op jit(solution)/shard_map/ppermute | solution.py:33
  34.1 0.8 copy-start
  42.8 9.2 %collective-permute-start.9 = (f32[4,32,512]{2,1,0:T(8,128)S(1)}, f32[4,32,512]{2,1,0:T(8,128)S(1)}, u32[]{:S(2)}, u32[]{:S(2)}) collective-permute-start(f32[4,32,512]{2,1,0:T(8,128)S(1)} %get-tuple-element.27), channel_id=1, source_target_pairs={{0,16},{1,17},{2,18},{3,19},{4,20},{5,21},{6,22},{7,23},{8,24},{9,... | collective-permute-start | bytes 786440 | tf_op jit(solution)/shard_map/ppermute | solution.py:33
  44.3 11.7 %collective-permute-start.10 = (f32[4,32,512]{2,1,0:T(8,128)S(1)}, f32[4,32,512]{2,1,0:T(8,128)S(1)}, u32[]{:S(2)}, u32[]{:S(2)}) collective-permute-start(f32[4,32,512]{2,1,0:T(8,128)S(1)} %get-tuple-element.28), channel_id=1, source_target_pairs={{0,24},{1,25},{2,26},{3,27},{4,28},{5,29},{6,30},{7,31},{8,16},{9,... | collective-permute-start | bytes 786440 | tf_op jit(solution)/shard_map/ppermute | solution.py:33
  44.4 11.7 %collective-permute-start.8 = (f32[4,32,512]{2,1,0:T(8,128)S(1)}, f32[4,32,512]{2,1,0:T(8,128)S(1)}, u32[]{:S(2)}, u32[]{:S(2)}) collective-permute-start(f32[4,32,512]{2,1,0:T(8,128)S(1)} %get-tuple-element.25), channel_id=1, source_target_pairs={{0,8},{1,9},{2,10},{3,11},{4,12},{5,13},{6,14},{7,15},{8,0},{9,1},... | collective-permute-start | bytes 786440 | tf_op jit(solution)/shard_map/ppermute | solution.py:33
  57.4 1.5 %collective-permute-start.11 = (f32[72,128]{1,0:T(8,128)S(1)}, f32[72,128]{1,0:T(8,128)S(1)}, u32[]{:S(2)}, u32[]{:S(2)}) collective-permute-start(f32[72,128]{1,0:T(8,128)S(1)} %product.1), channel_id=1, source_target_pairs={{0,8},{1,9},{2,10},{3,11},{4,12},{5,13},{6,14},{7,15},{8,0},{9,1},... | collective-permute-start | bytes 110600 | tf_op jit(solution)/shard_map/ppermute | solution.py:33
  58.9 4.9 %collective-permute-start.14 = (f32[72,128]{1,0:T(8,128)S(1)}, f32[72,128]{1,0:T(8,128)S(1)}, u32[]{:S(2)}, u32[]{:S(2)}) collective-permute-start(f32[72,128]{1,0:T(8,128)S(1)} %add.49), channel_id=1, source_target_pairs={{0,17},{1,16},{2,19},{3,18},{4,21},{5,20},{6,23},{7,22},{8,25},{9,... | collective-permute-start | bytes 110600 | tf_op jit(solution)/shard_map/ppermute | solution.py:33
  60.5 4.0 %collective-permute-start.13 = (f32[72,128]{1,0:T(8,128)S(1)}, f32[72,128]{1,0:T(8,128)S(1)}, u32[]{:S(2)}, u32[]{:S(2)}) collective-permute-start(f32[72,128]{1,0:T(8,128)S(1)} %add.49), channel_id=1, source_target_pairs={{0,1},{1,0},{2,3},{3,2},{4,5},{5,4},{6,7},{7,6},{8,9},{9,8},{10,11... | collective-permute-start | bytes 110600 | tf_op jit(solution)/shard_map/ppermute | solution.py:33
  61.9 4.0 %collective-permute-start.12 = (f32[72,128]{1,0:T(8,128)S(1)}, f32[72,128]{1,0:T(8,128)S(1)}, u32[]{:S(2)}, u32[]{:S(2)}) collective-permute-start(f32[72,128]{1,0:T(8,128)S(1)} %add.49), channel_id=1, source_target_pairs={{0,16},{1,17},{2,18},{3,19},{4,20},{5,21},{6,22},{7,23},{8,24},{9,... | collective-permute-start | bytes 110600 | tf_op jit(solution)/shard_map/ppermute | solution.py:33
  65.9 5.9 %collective-permute-start.17 = (f32[72,128]{1,0:T(8,128)S(1)}, f32[72,128]{1,0:T(8,128)S(1)}, u32[]{:S(2)}, u32[]{:S(2)}) collective-permute-start(f32[72,128]{1,0:T(8,128)S(1)} %add_add_fusion.3), channel_id=1, source_target_pairs={{0,6},{1,7},{2,4},{3,5},{4,2},{5,3},{6,0},{7,1},{8,14},{9,15},{10,... | collective-permute-start | bytes 110600 | tf_op jit(solution)/shard_map/ppermute | solution.py:33
  68.6 4.9 %collective-permute-start.16 = (f32[72,128]{1,0:T(8,128)S(1)}, f32[72,128]{1,0:T(8,128)S(1)}, u32[]{:S(2)}, u32[]{:S(2)}) collective-permute-start(f32[72,128]{1,0:T(8,128)S(1)} %add_add_fusion.3), channel_id=1, source_target_pairs={{0,4},{1,5},{2,6},{3,7},{4,0},{5,1},{6,2},{7,3},{8,12},{9,13},{10,... | collective-permute-start | bytes 110600 | tf_op jit(solution)/shard_map/ppermute | solution.py:33
  68.6 4.9 %collective-permute-start.15 = (f32[72,128]{1,0:T(8,128)S(1)}, f32[72,128]{1,0:T(8,128)S(1)}, u32[]{:S(2)}, u32[]{:S(2)}) collective-permute-start(f32[72,128]{1,0:T(8,128)S(1)} %add_add_fusion.3), channel_id=1, source_target_pairs={{0,2},{1,3},{2,0},{3,1},{4,6},{5,7},{6,4},{7,5},{8,10},{9,11},{10,... | collective-permute-start | bytes 110600 | tf_op jit(solution)/shard_map/ppermute | solution.py:33

commit v5 on v4

--- a/solution.py
+++ b/solution.py
@@ -74,6 +74,9 @@
     def column(tile, c):
         return jnp.broadcast_to(tile[:, c : c + 1], (SUBLANES, LANES))
 
+    def spread(tile, r):
+        return jnp.take_along_axis(tile, jnp.full(tile.shape, r, jnp.int32), axis=0)
+
     def less(tile, factor, other):
         return tile - factor[:, : tile.shape[1]] * other
 
@@ -81,9 +84,8 @@
         at, first = divmod(g * SUBLANES, LANES)
         both = [gram[h] + extra[h] for h in range(len(gram))]
         rows = [[row(t, q) for t in both[g]] for q in range(SUBLANES)]
-        block = [
-            [column(rows[a][at], first + b) if b >= a else None for b in range(SUBLANES)] for a in range(SUBLANES)
-        ]
+        pivots = [column(gram[g][at], first + b) for b in range(SUBLANES)]
+        block = [[spread(pivots[b], a) if b >= a else None for b in range(SUBLANES)] for a in range(SUBLANES)]
         below = range(g + 1, len(gram))
         columns = {h: [column(gram[h][at], first + q) for q in range(SUBLANES)] for h in below}
         scales, inverses = [], []
@@ -277,43 +279,32 @@
     )(basis, gram)
 
 
-def ahead_kernel(chunks, species, place, field, image, *refs):
-    outs, narrow = refs[:-1], refs[-1]
-    half = len(outs)
-    share, x_cells, width = outs[0].shape
+def ahead_kernel(d, species, place, field, image, out, narrow):
+    share, x_cells, width = out.shape
     rank = image.shape[0]
-    across = half * share * species
-    far = 1 - place[0] // half
-    start = pl.multiple_of(far * across, across)
-    step = x_cells // chunks
-    weights = species_weights(image[...], LANES // rank)
-    for i in range(chunks):
-        cells = field[i * step : (i + 1) * step, pl.ds(start, across), :]
-        narrow[...] = times(cells.reshape(step * across, cells.shape[2]), weights)
-        for d, out in enumerate(outs):
-            place_of_d = (place[0] ^ d) & (half - 1)
-            for y in range(share):
-                first = pl.multiple_of((place_of_d * share + y) * species, species)
-                for t in range(width // LANES):
-                    out[y, i * step : (i + 1) * step, t * LANES : (t + 1) * LANES] = packed(
-                        narrow, first + t * (LANES // rank), step, across, rank
-                    )
-
-
-def contract_ahead(place, field, image, x_cells, y_cells, species, x_parts):
+    across = share * species
+    start = pl.multiple_of((place[0] ^ d) * across, across)
+    cells = field[:, pl.ds(start, across), :]
+    narrow[...] = times(cells.reshape(x_cells * across, cells.shape[2]), species_weights(image[...], LANES // rank))
+    for y in range(share):
+        for t in range(width // LANES):
+            out[y, :, t * LANES : (t + 1) * LANES] = packed(
+                narrow, y * species + t * (LANES // rank), x_cells, across, rank
+            )
+
+
+def contract_ahead(place, field, image, x_cells, y_cells, species, x_parts, d):
     z = field.shape[1]
     rank = image.shape[0]
-    chunks = 2
-    across = y_cells // 2 * species
-    piece = jax.ShapeDtypeStruct((y_cells // x_parts, x_cells, species * rank), F32)
-    return pl.pallas_call(
-        functools.partial(ahead_kernel, chunks, species),
-        out_shape=[piece] * (x_parts // 2),
+    share = y_cells // x_parts
+    return pl.pallas_call(
+        functools.partial(ahead_kernel, d, species),
+        out_shape=jax.ShapeDtypeStruct((share, x_cells, species * rank), F32),
         in_specs=[SMEM, VMEM, VMEM],
-        out_specs=[VMEM] * (x_parts // 2),
-        scratch_shapes=[pltpu.VMEM((x_cells // chunks * across, LANES), F32)],
-        compiler_params=SMALL,
-        name="ahead",
+        out_specs=VMEM,
+        scratch_shapes=[pltpu.VMEM((x_cells * share * species, LANES), F32)],
+        compiler_params=SMALL,
+        cost_estimate=pl.CostEstimate(flops=1 << 30, bytes_accessed=1 << 22, transcendentals=0),
     )(place, field.reshape(x_cells, y_cells * species, z), image)
 
 
@@ -460,8 +451,10 @@
     mine = summed(mine + partner(other, 1))
     other = partner(mine, 1)
     basis, image, gram = begin(place, mine, other, start_basis.T)
-    ahead = contract_ahead(place, held, image, x_cells, y_cells, species, x_parts)
-    far = [partner(piece, d + x_parts // 2) for d, piece in enumerate(ahead)]
+    far = []
+    for d in range(x_parts // 2, x_parts):
+        piece = contract_ahead(place, held, image, x_cells, y_cells, species, x_parts, d)
+        far.append(partner(piece, d))
     basis_rows, factor = finish(basis, gram)
     core_tensor, *near = contract(place, held, basis_rows, x_cells, y_cells, species, x_parts)
     near = [partner(piece, d) if d else piece for d, piece in enumerate(near)]

time: 78.4 us -> 76.7 us (0.978)
  Pallas kernels: 26.9 us -> 24.9 us
  waiting for transfers between devices: 29.5 us -> 30.3 us
    pallas_call x1, Pallas kernels: 4.8 us -> 3.95 us  [triangle(): pl.pallas_call(functools.partial(triangle_kernel, scale), out_shape=jax.S...]
    ppermute x18, waiting for transfers between devices: 29.5 us -> 30.3 us  [partner(): return lax.ppermute(value, ('gx', 'gy'), pairs)]
    pallas_call x1 -> x2, Pallas kernels: 3.48 us -> 3.13 us  [contract_ahead(): pl.pallas_call(functools.partial(ahead_kernel, d, species), out_shape=jax...]
where the time goes in v5:
time: 76.7 us; the launch traced here: 76.5 us
  waiting for transfers between devices  30.3 us (40%)
  Pallas kernels  24.9 us (32%)
  starting transfers between devices  19.8 us (26%)
    ppermute x18, waiting for transfers between devices, partner(): return lax.ppermute(value, ('gx', 'gy'), pairs)  30.3 us
    ppermute x18, starting transfers between devices, partner(): return lax.ppermute(value, ('gx', 'gy'), pairs)  19.8 us
    pallas_call x1, Pallas kernels, local_gram(): pl.pallas_call(functools.partial(gram_kernel, cuts), out_shape=[out, out,...  4.99 us
    pallas_call x1, Pallas kernels, contract(): pl.pallas_call(functools.partial(core_kernel, species, y_cells), grid=(st...  4.43 us
    pallas_call x1, Pallas kernels, triangle(): pl.pallas_call(functools.partial(triangle_kernel, scale), out_shape=jax.S...  3.95 us
    pallas_call x1, Pallas kernels, finish(): pl.pallas_call(finish_kernel, out_shape=[jax.ShapeDtypeStruct((rank, z),...  3.52 us
    pallas_call x1, Pallas kernels, begin(): pl.pallas_call(begin_kernel, out_shape=[rows, rows, jax.ShapeDtypeStruct(...  3.5 us
    pallas_call x2, Pallas kernels, contract_ahead(): pl.pallas_call(functools.partial(ahead_kernel, d, species), out_shape=jax...  3.13 us
  transfers between devices with their start and end apart: 18, of which 15 were waited for; matrix products, arithmetic and copies ran while one was open for 0% of the time, Pallas kernels for 0%

profile of v5, /device:TPU:0, one launch (start us, length us, event | category | flops | bytes accessed | tf_op | source)
XLA Modules:
  0.0 76.5 jit_solution(9798961318709425085)
XLA Ops:
  0.6 0.0 copy-start.1
  0.6 5.0 %gram.1 = (f32[136,128]{1,0:T(8,128)S(1)}, f32[136,128]{1,0:T(8,128)S(1)}, f32[8192,256]{1,0:T(8,128)S(1)}) custom-call(s32[1]{0:T(128)} %bitcast.place, f32[8192,256]{1,0:T(8,128)} %bitcast.10), custom_call_target="tpu_custom_call" | custom-call | tf_op jit(solution)/shard_map/gram/pallas_call | solution.py:210
  5.6 0.6 collective-permute-start
  6.2 0.9 %collective-permute-done = f32[136,128]{1,0:T(8,128)S(1)} collective-permute-done((f32[136,128]{1,0:T(8,128)S(1)}, f32[136,128]{1,0:T(8,128)S(1)}, u32[]{:S(2)}, u32[]{:S(2)}) %collective-permute-start) | collective-permute-done | bytes 69664 | tf_op jit(solution)/shard_map/ppermute | solution.py:33
  7.1 3.8 %collective-permute-start.3 = (f32[136,128]{1,0:T(8,128)S(1)}, f32[136,128]{1,0:T(8,128)S(1)}, u32[]{:S(2)}, u32[]{:S(2)}) collective-permute-start(f32[136,128]{1,0:T(8,128)S(1)} %add.42), channel_id=1, source_target_pairs={{0,17},{1,16},{2,19},{3,18},{4,21},{5,20},{6,23},{7,22},{8,25},{9,... | collective-permute-start | bytes 208904 | tf_op jit(solution)/shard_map/ppermute | solution.py:33
  11.0 0.5 collective-permute-start.2
  11.5 0.1 collective-permute-start.1
  11.6 1.9 %collective-permute-done.3 = f32[136,128]{1,0:T(8,128)S(1)} collective-permute-done((f32[136,128]{1,0:T(8,128)S(1)}, f32[136,128]{1,0:T(8,128)S(1)}, u32[]{:S(2)}, u32[]{:S(2)}) %collective-permute-start.3) | collective-permute-done | bytes 69664 | tf_op jit(solution)/shard_map/ppermute | solution.py:33
  13.5 1.8 %collective-permute-done.2 = f32[136,128]{1,0:T(8,128)S(1)} collective-permute-done((f32[136,128]{1,0:T(8,128)S(1)}, f32[136,128]{1,0:T(8,128)S(1)}, u32[]{:S(2)}, u32[]{:S(2)}) %collective-permute-start.2) | collective-permute-done | bytes 69664 | tf_op jit(solution)/shard_map/ppermute | solution.py:33
  15.3 0.5 collective-permute-done.1
  15.8 3.7 %collective-permute-start.6 = (f32[136,128]{1,0:T(8,128)S(1)}, f32[136,128]{1,0:T(8,128)S(1)}, u32[]{:S(2)}, u32[]{:S(2)}) collective-permute-start(f32[136,128]{1,0:T(8,128)S(1)} %add_add_fusion.1), channel_id=1, source_target_pairs={{0,6},{1,7},{2,4},{3,5},{4,2},{5,3},{6,0},{7,1},{8,14},{9,15},{10,... | collective-permute-start | bytes 208904 | tf_op jit(solution)/shard_map/ppermute | solution.py:33
  19.5 0.0 collective-permute-start.5
  19.5 0.8 %collective-permute-start.4 = (f32[136,128]{1,0:T(8,128)S(1)}, f32[136,128]{1,0:T(8,128)S(1)}, u32[]{:S(2)}, u32[]{:S(2)}) collective-permute-start(f32[136,128]{1,0:T(8,128)S(1)} %add_add_fusion.1), channel_id=1, source_target_pairs={{0,2},{1,3},{2,0},{3,1},{4,6},{5,7},{6,4},{7,5},{8,10},{9,11},{10,... | collective-permute-start | bytes 208904 | tf_op jit(solution)/shard_map/ppermute | solution.py:33
  20.3 1.9 %collective-permute-done.6 = f32[136,128]{1,0:T(8,128)S(1)} collective-permute-done((f32[136,128]{1,0:T(8,128)S(1)}, f32[136,128]{1,0:T(8,128)S(1)}, u32[]{:S(2)}, u32[]{:S(2)}) %collective-permute-start.6) | collective-permute-done | bytes 69664 | tf_op jit(solution)/shard_map/ppermute | solution.py:33
  22.1 2.8 %collective-permute-done.5 = f32[136,128]{1,0:T(8,128)S(1)} collective-permute-done((f32[136,128]{1,0:T(8,128)S(1)}, f32[136,128]{1,0:T(8,128)S(1)}, u32[]{:S(2)}, u32[]{:S(2)}) %collective-permute-start.5) | collective-permute-done | bytes 69664 | tf_op jit(solution)/shard_map/ppermute | solution.py:33
  24.9 0.0 collective-permute-done.4
  24.9 0.1 collective-permute-start.7
  25.0 1.2 %collective-permute-done.7.other = f32[136,128]{1,0:T(8,128)S(1)} collective-permute-done((f32[136,128]{1,0:T(8,128)S(1)}, f32[136,128]{1,0:T(8,128)S(1)}, u32[]{:S(2)}, u32[]{:S(2)}) %collective-permute-start.7) | collective-permute-done | bytes 69664 | tf_op jit(solution)/shard_map/ppermute | solution.py:33
  26.3 0.0 copy-done.1
  26.3 3.5 %begin.1 = (f32[32,256]{1,0:T(8,128)S(1)}, f32[32,256]{1,0:T(8,128)S(1)}, f32[256,256]{1,0:T(8,128)S(1)}) custom-call(s32[1]{0:T(128)} %bitcast.place, f32[136,128]{1,0:T(8,128)S(1)} %add_add_fusion.mine, f32[136,128]{1,0:T(8,128)S(1)} %collective-permute-done.7.other, f32[32,256]{1,0:T(8,128)S(1)} %bitcast.9), custom_call_target="tpu_custom_call" | custom-call | tf_op jit(solution)/shard_map/begin/pallas_call | solution.py:248
  29.8 1.6 %shard_map.50 = f32[4,32,512]{2,1,0:T(8,128)S(1)} custom-call(s32[1]{0:T(128)} %bitcast.place, f32[32,256,256]{2,1,0:T(8,128)S(1)} %bitcast.6, f32[32,256]{1,0:T(8,128)S(1)} %get-tuple-element.24.image), custom_call_target="tpu_custom_call" | custom-call | flops 1073741824 | bytes 4194304 | tf_op jit(solution)/shard_map/pallas_call | solution.py:300
  31.3 1.6 %shard_map.49 = f32[4,32,512]{2,1,0:T(8,128)S(1)} custom-call(s32[1]{0:T(128)} %bitcast.place, f32[32,256,256]{2,1,0:T(8,128)S(1)} %bitcast.7, f32[32,256]{1,0:T(8,128)S(1)} %get-tuple-element.24.image), custom_call_target="tpu_custom_call" | custom-call | flops 1073741824 | bytes 4194304 | tf_op jit(solution)/shard_map/pallas_call | solution.py:300
  32.9 3.5 %finish.1 = (f32[32,256]{1,0:T(8,128)}, f32[32,32]{1,0:T(8,128)S(1)}) custom-call(f32[32,256]{1,0:T(8,128)S(1)} %get-tuple-element.17.basis, f32[256,256]{1,0:T(8,128)S(1)} %get-tuple-element.18.gram), custom_call_target="tpu_custom_call" | custom-call | flops 1073741824 | bytes 16777216 | tf_op jit(solution)/shard_map/finish/pallas_call | solution.py:271
  36.4 0.0 copy-start
  36.4 0.8 copy-done
  37.2 4.4 %core.1 = (f32[512,512]{1,0:T(8,128)}, f32[4,32,512]{2,1,0:T(8,128)S(1)}, f32[4,32,512]{2,1,0:T(8,128)S(1)}) custom-call(s32[1]{0:T(128)} %bitcast.place, f32[8192,256]{1,0:T(8,128)S(1)} %get-tuple-element.14.field, f32[32,256]{1,0:T(8,128)S(1)} %copy-done), custom_call_target="tpu_custom_call" | custom-call | flops 2147483648 | bytes 16777216 | tf_op jit(solution)/shard_map/core/pallas_call | solution.py:343
  41.6 0.2 collective-permute-start.8
  41.8 1.5 %collective-permute-start.9 = (f32[4,32,512]{2,1,0:T(8,128)S(1)}, f32[4,32,512]{2,1,0:T(8,128)S(1)}, u32[]{:S(2)}, u32[]{:S(2)}) collective-permute-start(f32[4,32,512]{2,1,0:T(8,128)S(1)} %shard_map.49), channel_id=1, source_target_pairs={{0,16},{1,17},{2,18},{3,19},{4,20},{5,21},{6,22},{7,23},{8,24},{9,... | collective-permute-start | bytes 786440 | tf_op jit(solution)/shard_map/ppermute | solution.py:33
  43.3 0.2 collective-permute-start.10
  43.5 0.0 collective-permute-done.8.refs_1_
  43.5 7.5 %collective-permute-done.9.refs_2_ = f32[4,32,512]{2,1,0:T(8,128)S(1)} collective-permute-done((f32[4,32,512]{2,1,0:T(8,128)S(1)}, f32[4,32,512]{2,1,0:T(8,128)S(1)}, u32[]{:S(2)}, u32[]{:S(2)}) %collective-permute-start.9) | collective-permute-done | bytes 262176 | tf_op jit(solution)/shard_map/ppermute | solution.py:33
  51.0 4.4 %collective-permute-done.10.refs_3_ = f32[4,32,512]{2,1,0:T(8,128)S(1)} collective-permute-done((f32[4,32,512]{2,1,0:T(8,128)S(1)}, f32[4,32,512]{2,1,0:T(8,128)S(1)}, u32[]{:S(2)}, u32[]{:S(2)}) %collective-permute-start.10) | collective-permute-done | bytes 262176 | tf_op jit(solution)/shard_map/ppermute | solution.py:33
  55.3 1.4 %product.1 = f32[72,128]{1,0:T(8,128)S(1)} custom-call(s32[1]{0:T(128)} %bitcast.place, f32[32,32]{1,0:T(8,128)S(1)} %get-tuple-element.21.factor, f32[4,32,512]{2,1,0:T(8,128)S(1)} %get-tuple-element.22.refs_0_, f32[4,32,512]{2,1,0:T(8,128)S(1)} %collective-permute-done.8.refs_1_, f32[4,32,512]{2,1,0:T(8,128)S(1)} %collective-permute-done.9.refs_2_, ...), custom_call_target="tpu_custom_call" | custom-call | tf_op jit(solution)/shard_map/product/pallas_call | solution.py:413
  56.7 0.4 collective-permute-start.11
  57.2 0.9 %collective-permute-done.11 = f32[72,128]{1,0:T(8,128)S(1)} collective-permute-done((f32[72,128]{1,0:T(8,128)S(1)}, f32[72,128]{1,0:T(8,128)S(1)}, u32[]{:S(2)}, u32[]{:S(2)}) %collective-permute-start.11) | collective-permute-done | bytes 36896 | tf_op jit(solution)/shard_map/ppermute | solution.py:33
  58.0 1.5 %collective-permute-start.14 = (f32[72,128]{1,0:T(8,128)S(1)}, f32[72,128]{1,0:T(8,128)S(1)}, u32[]{:S(2)}, u32[]{:S(2)}) collective-permute-start(f32[72,128]{1,0:T(8,128)S(1)} %add.49), channel_id=1, source_target_pairs={{0,17},{1,16},{2,19},{3,18},{4,21},{5,20},{6,23},{7,22},{8,25},{9,... | collective-permute-start | bytes 110600 | tf_op jit(solution)/shard_map/ppermute | solution.py:33
  59.6 1.5 %collective-permute-start.13 = (f32[72,128]{1,0:T(8,128)S(1)}, f32[72,128]{1,0:T(8,128)S(1)}, u32[]{:S(2)}, u32[]{:S(2)}) collective-permute-start(f32[72,128]{1,0:T(8,128)S(1)} %add.49), channel_id=1, source_target_pairs={{0,1},{1,0},{2,3},{3,2},{4,5},{5,4},{6,7},{7,6},{8,9},{9,8},{10,11... | collective-permute-start | bytes 110600 | tf_op jit(solution)/shard_map/ppermute | solution.py:33
  61.0 0.5 collective-permute-start.12
  61.5 1.4 %collective-permute-done.14 = f32[72,128]{1,0:T(8,128)S(1)} collective-permute-done((f32[72,128]{1,0:T(8,128)S(1)}, f32[72,128]{1,0:T(8,128)S(1)}, u32[]{:S(2)}, u32[]{:S(2)}) %collective-permute-start.14) | collective-permute-done | bytes 36896 | tf_op jit(solution)/shard_map/ppermute | solution.py:33
  62.9 0.6 collective-permute-done.13
  63.5 1.5 %collective-permute-done.12 = f32[72,128]{1,0:T(8,128)S(1)} collective-permute-done((f32[72,128]{1,0:T(8,128)S(1)}, f32[72,128]{1,0:T(8,128)S(1)}, u32[]{:S(2)}, u32[]{:S(2)}) %collective-permute-start.12) | collective-permute-done | bytes 36896 | tf_op jit(solution)/shard_map/ppermute | solution.py:33
  65.0 2.7 %collective-permute-start.17 = (f32[72,128]{1,0:T(8,128)S(1)}, f32[72,128]{1,0:T(8,128)S(1)}, u32[]{:S(2)}, u32[]{:S(2)}) collective-permute-start(f32[72,128]{1,0:T(8,128)S(1)} %add_add_fusion.3), channel_id=1, source_target_pairs={{0,6},{1,7},{2,4},{3,5},{4,2},{5,3},{6,0},{7,1},{8,14},{9,15},{10,... | collective-permute-start | bytes 110600 | tf_op jit(solution)/shard_map/ppermute | solution.py:33
  67.7 0.0 collective-permute-start.16
  67.7 1.7 %collective-permute-start.15 = (f32[72,128]{1,0:T(8,128)S(1)}, f32[72,128]{1,0:T(8,128)S(1)}, u32[]{:S(2)}, u32[]{:S(2)}) collective-permute-start(f32[72,128]{1,0:T(8,128)S(1)} %add_add_fusion.3), channel_id=1, source_target_pairs={{0,2},{1,3},{2,0},{3,1},{4,6},{5,7},{6,4},{7,5},{8,10},{9,11},{10,... | collective-permute-start | bytes 110600 | tf_op jit(solution)/shard_map/ppermute | solution.py:33
  69.5 1.4 %collective-permute-done.17 = f32[72,128]{1,0:T(8,128)S(1)} collective-permute-done((f32[72,128]{1,0:T(8,128)S(1)}, f32[72,128]{1,0:T(8,128)S(1)}, u32[]{:S(2)}, u32[]{:S(2)}) %collective-permute-start.17) | collective-permute-done | bytes 36896 | tf_op jit(solution)/shard_map/ppermute | solution.py:33
  70.9 1.7 %collective-permute-done.16 = f32[72,128]{1,0:T(8,128)S(1)} collective-permute-done((f32[72,128]{1,0:T(8,128)S(1)}, f32[72,128]{1,0:T(8,128)S(1)}, u32[]{:S(2)}, u32[]{:S(2)}) %collective-permute-start.16) | collective-permute-done | bytes 36896 | tf_op jit(solution)/shard_map/ppermute | solution.py:33
  72.6 0.0 collective-permute-done.15
  72.6 3.9 %triangle.1 = f32[128,128]{1,0:T(8,128)} custom-call(f32[72,128]{1,0:T(8,128)S(1)} %add_add_fusion.2.gram), custom_call_target="tpu_custom_call" | custom-call | tf_op jit(solution)/shard_map/triangle/pallas_call | solution.py:434
  (6 shorter events, 0.1 us)
Async XLA Ops:
  0.6 25.6 %copy-start.1 = (f32[256,32]{0,1:T(8,128)S(1)}, f32[256,32]{0,1:T(8,128)}, u32[]{:S(2)}) copy-start(f32[256,32]{0,1:T(8,128)} %param.3) | copy-start | bytes 98308
  5.6 1.5 %collective-permute-start = (f32[136,128]{1,0:T(8,128)S(1)}, f32[136,128]{1,0:T(8,128)S(1)}, u32[]{:S(2)}, u32[]{:S(2)}) collective-permute-start(f32[136,128]{1,0:T(8,128)S(1)} %get-tuple-element.16), channel_id=1, source_target_pairs={{0,8},{1,9},{2,10},{3,11},{4,12},{5,13},{6,14},{7,15},{8,0},{9,1},... | collective-permute-start | bytes 208904 | tf_op jit(solution)/shard_map/ppermute | solution.py:33
  7.1 6.3 %collective-permute-start.3 = (f32[136,128]{1,0:T(8,128)S(1)}, f32[136,128]{1,0:T(8,128)S(1)}, u32[]{:S(2)}, u32[]{:S(2)}) collective-permute-start(f32[136,128]{1,0:T(8,128)S(1)} %add.42), channel_id=1, source_target_pairs={{0,17},{1,16},{2,19},{3,18},{4,21},{5,20},{6,23},{7,22},{8,25},{9,... | collective-permute-start | bytes 208904 | tf_op jit(solution)/shard_map/ppermute | solution.py:33
  11.0 4.3 %collective-permute-start.2 = (f32[136,128]{1,0:T(8,128)S(1)}, f32[136,128]{1,0:T(8,128)S(1)}, u32[]{:S(2)}, u32[]{:S(2)}) collective-permute-start(f32[136,128]{1,0:T(8,128)S(1)} %add.42), channel_id=1, source_target_pairs={{0,1},{1,0},{2,3},{3,2},{4,5},{5,4},{6,7},{7,6},{8,9},{9,8},{10,11... | collective-permute-start | bytes 208904 | tf_op jit(solution)/shard_map/ppermute | solution.py:33
  11.5 4.3 %collective-permute-start.1 = (f32[136,128]{1,0:T(8,128)S(1)}, f32[136,128]{1,0:T(8,128)S(1)}, u32[]{:S(2)}, u32[]{:S(2)}) collective-permute-start(f32[136,128]{1,0:T(8,128)S(1)} %add.42), channel_id=1, source_target_pairs={{0,16},{1,17},{2,18},{3,19},{4,20},{5,21},{6,22},{7,23},{8,24},{9,... | collective-permute-start | bytes 208904 | tf_op jit(solution)/shard_map/ppermute | solution.py:33
  15.8 6.3 %collective-permute-start.6 = (f32[136,128]{1,0:T(8,128)S(1)}, f32[136,128]{1,0:T(8,128)S(1)}, u32[]{:S(2)}, u32[]{:S(2)}) collective-permute-start(f32[136,128]{1,0:T(8,128)S(1)} %add_add_fusion.1), channel_id=1, source_target_pairs={{0,6},{1,7},{2,4},{3,5},{4,2},{5,3},{6,0},{7,1},{8,14},{9,15},{10,... | collective-permute-start | bytes 208904 | tf_op jit(solution)/shard_map/ppermute | solution.py:33
  19.5 5.5 %collective-permute-start.5 = (f32[136,128]{1,0:T(8,128)S(1)}, f32[136,128]{1,0:T(8,128)S(1)}, u32[]{:S(2)}, u32[]{:S(2)}) collective-permute-start(f32[136,128]{1,0:T(8,128)S(1)} %add_add_fusion.1), channel_id=1, source_target_pairs={{0,4},{1,5},{2,6},{3,7},{4,0},{5,1},{6,2},{7,3},{8,12},{9,13},{10,... | collective-permute-start | bytes 208904 | tf_op jit(solution)/shard_map/ppermute | solution.py:33
  19.5 5.5 %collective-permute-start.4 = (f32[136,128]{1,0:T(8,128)S(1)}, f32[136,128]{1,0:T(8,128)S(1)}, u32[]{:S(2)}, u32[]{:S(2)}) collective-permute-start(f32[136,128]{1,0:T(8,128)S(1)} %add_add_fusion.1), channel_id=1, source_target_pairs={{0,2},{1,3},{2,0},{3,1},{4,6},{5,7},{6,4},{7,5},{8,10},{9,11},{10,... | collective-permute-start | bytes 208904 | tf_op jit(solution)/shard_map/ppermute | solution.py:33
  24.9 1.3 %collective-permute-start.7 = (f32[136,128]{1,0:T(8,128)S(1)}, f32[136,128]{1,0:T(8,128)S(1)}, u32[]{:S(2)}, u32[]{:S(2)}) collective-permute-start(f32[136,128]{1,0:T(8,128)S(1)} %add_add_fusion.mine), channel_id=1, source_target_pairs={{0,8},{1,9},{2,10},{3,11},{4,12},{5,13},{6,14},{7,15},{8,0},{9,1},... | collective-permute-start | bytes 208904 | tf_op jit(solution)/shard_map/ppermute | solution.py:33
  36.4 0.8 copy-start
  41.6 1.9 %collective-permute-start.8 = (f32[4,32,512]{2,1,0:T(8,128)S(1)}, f32[4,32,512]{2,1,0:T(8,128)S(1)}, u32[]{:S(2)}, u32[]{:S(2)}) collective-permute-start(f32[4,32,512]{2,1,0:T(8,128)S(1)} %get-tuple-element.23), channel_id=1, source_target_pairs={{0,8},{1,9},{2,10},{3,11},{4,12},{5,13},{6,14},{7,15},{8,0},{9,1},... | collective-permute-start | bytes 786440 | tf_op jit(solution)/shard_map/ppermute | solution.py:33
  41.8 9.2 %collective-permute-start.9 = (f32[4,32,512]{2,1,0:T(8,128)S(1)}, f32[4,32,512]{2,1,0:T(8,128)S(1)}, u32[]{:S(2)}, u32[]{:S(2)}) collective-permute-start(f32[4,32,512]{2,1,0:T(8,128)S(1)} %shard_map.49), channel_id=1, source_target_pairs={{0,16},{1,17},{2,18},{3,19},{4,20},{5,21},{6,22},{7,23},{8,24},{9,... | collective-permute-start | bytes 786440 | tf_op jit(solution)/shard_map/ppermute | solution.py:33
  43.3 12.0 %collective-permute-start.10 = (f32[4,32,512]{2,1,0:T(8,128)S(1)}, f32[4,32,512]{2,1,0:T(8,128)S(1)}, u32[]{:S(2)}, u32[]{:S(2)}) collective-permute-start(f32[4,32,512]{2,1,0:T(8,128)S(1)} %shard_map.50), channel_id=1, source_target_pairs={{0,24},{1,25},{2,26},{3,27},{4,28},{5,29},{6,30},{7,31},{8,16},{9,... | collective-permute-start | bytes 786440 | tf_op jit(solution)/shard_map/ppermute | solution.py:33
  56.7 1.3 %collective-permute-start.11 = (f32[72,128]{1,0:T(8,128)S(1)}, f32[72,128]{1,0:T(8,128)S(1)}, u32[]{:S(2)}, u32[]{:S(2)}) collective-permute-start(f32[72,128]{1,0:T(8,128)S(1)} %product.1), channel_id=1, source_target_pairs={{0,8},{1,9},{2,10},{3,11},{4,12},{5,13},{6,14},{7,15},{8,0},{9,1},... | collective-permute-start | bytes 110600 | tf_op jit(solution)/shard_map/ppermute | solution.py:33
  58.0 4.9 %collective-permute-start.14 = (f32[72,128]{1,0:T(8,128)S(1)}, f32[72,128]{1,0:T(8,128)S(1)}, u32[]{:S(2)}, u32[]{:S(2)}) collective-permute-start(f32[72,128]{1,0:T(8,128)S(1)} %add.49), channel_id=1, source_target_pairs={{0,17},{1,16},{2,19},{3,18},{4,21},{5,20},{6,23},{7,22},{8,25},{9,... | collective-permute-start | bytes 110600 | tf_op jit(solution)/shard_map/ppermute | solution.py:33
  59.6 4.0 %collective-permute-start.13 = (f32[72,128]{1,0:T(8,128)S(1)}, f32[72,128]{1,0:T(8,128)S(1)}, u32[]{:S(2)}, u32[]{:S(2)}) collective-permute-start(f32[72,128]{1,0:T(8,128)S(1)} %add.49), channel_id=1, source_target_pairs={{0,1},{1,0},{2,3},{3,2},{4,5},{5,4},{6,7},{7,6},{8,9},{9,8},{10,11... | collective-permute-start | bytes 110600 | tf_op jit(solution)/shard_map/ppermute | solution.py:33
  61.0 4.0 %collective-permute-start.12 = (f32[72,128]{1,0:T(8,128)S(1)}, f32[72,128]{1,0:T(8,128)S(1)}, u32[]{:S(2)}, u32[]{:S(2)}) collective-permute-start(f32[72,128]{1,0:T(8,128)S(1)} %add.49), channel_id=1, source_target_pairs={{0,16},{1,17},{2,18},{3,19},{4,20},{5,21},{6,22},{7,23},{8,24},{9,... | collective-permute-start | bytes 110600 | tf_op jit(solution)/shard_map/ppermute | solution.py:33
  65.0 5.9 %collective-permute-start.17 = (f32[72,128]{1,0:T(8,128)S(1)}, f32[72,128]{1,0:T(8,128)S(1)}, u32[]{:S(2)}, u32[]{:S(2)}) collective-permute-start(f32[72,128]{1,0:T(8,128)S(1)} %add_add_fusion.3), channel_id=1, source_target_pairs={{0,6},{1,7},{2,4},{3,5},{4,2},{5,3},{6,0},{7,1},{8,14},{9,15},{10,... | collective-permute-start | bytes 110600 | tf_op jit(solution)/shard_map/ppermute | solution.py:33
  67.7 4.9 %collective-permute-start.16 = (f32[72,128]{1,0:T(8,128)S(1)}, f32[72,128]{1,0:T(8,128)S(1)}, u32[]{:S(2)}, u32[]{:S(2)}) collective-permute-start(f32[72,128]{1,0:T(8,128)S(1)} %add_add_fusion.3), channel_id=1, source_target_pairs={{0,4},{1,5},{2,6},{3,7},{4,0},{5,1},{6,2},{7,3},{8,12},{9,13},{10,... | collective-permute-start | bytes 110600 | tf_op jit(solution)/shard_map/ppermute | solution.py:33
  67.7 4.9 %collective-permute-start.15 = (f32[72,128]{1,0:T(8,128)S(1)}, f32[72,128]{1,0:T(8,128)S(1)}, u32[]{:S(2)}, u32[]{:S(2)}) collective-permute-start(f32[72,128]{1,0:T(8,128)S(1)} %add_add_fusion.3), channel_id=1, source_target_pairs={{0,2},{1,3},{2,0},{3,1},{4,6},{5,7},{6,4},{7,5},{8,10},{9,11},{10,... | collective-permute-start | bytes 110600 | tf_op jit(solution)/shard_map/ppermute | solution.py:33
